TPU v7x, 256 devices: a whole 4x4x8 slice. The times are simulated.
256 devices in a mesh: dp: 8 (over x, core), seq: 32 (over z, y).
Axes of the slice: x: 4, y: 4, z: 8, core: 2. Of those that a mesh axis runs over, the one named last changes fastest.
Arguments:
- projected: bfloat16 [8, 4096, 6144], P('dp', 'seq'), may hold values from -8 to 8
- out_weight: bfloat16 [2048, 2048], P(('dp', 'seq')), may hold values from -0.125 to 0.125
- upstream: bfloat16 [8, 4096, 2048], P('dp', 'seq'), may hold values from -6 to 6
- peak_mask: int32 [8, 4096], P('dp', 'seq'), may hold values 0 or 1
- block_layout: int32 [32, 32, 8], P('seq'), may hold values from 0 to 31, as said below
Outputs:
- attended: bfloat16 [8, 4096, 2048], P('dp', 'seq')
- projected_grad: bfloat16 [8, 4096, 6144], P('dp', 'seq')
- weight_grad: float32 [2048, 2048], P(('dp', 'seq'))
Inputs may be any that keep to these rules, and one draw needn't show every extreme that they name: `block_layout`: for each head and each block row of queries, 8 distinct key-block indices, one of which is the row's own block.
All inputs are finite; a program needn't handle non-finite values. No bound on the sum of `peak_mask` on one device may be relied on, other than what follows from the above.
Results may differ from a plain program's by a relative error of at most 0.019.
Values may be sent and summed in bfloat16 or wider, within the bound.
A program may use at most 128 MiB of HBM per device.

v0:
```python
import math

import jax
import jax.numpy as jnp
from jax import lax
from jax.sharding import PartitionSpec as P

HS = 64


def group_size(block_count, block_len):
    return math.gcd(block_count, max(1, 512 // block_len))


def block_forward(queries, key_rows, values, layout):
    seq_len, head_width = queries.shape
    block_count, key_count = layout.shape
    block_len = seq_len // block_count
    row_group = group_size(block_count, block_len)
    group_count = block_count // row_group
    score_scale = 1.0 / math.sqrt(head_width)
    key_blocks = key_rows.reshape(block_count, block_len, head_width)
    value_blocks = values.reshape(block_count, block_len, head_width)
    query_groups = queries.reshape(group_count, row_group, block_len, head_width)
    layout_groups = layout.reshape(group_count, row_group, key_count)

    def forward_group(packed):
        query_group, layout_group = packed
        key_group = key_blocks[layout_group].reshape(row_group, key_count * block_len, head_width)
        value_group = value_blocks[layout_group].reshape(
            row_group, key_count * block_len, head_width
        )
        scores = (
            jnp.einsum("gqd,gkd->gqk", query_group, key_group, preferred_element_type=jnp.float32)
            * score_scale
        )
        row_top = jnp.max(scores, axis=-1, keepdims=True)
        log_total = row_top + jnp.log(jnp.sum(jnp.exp(scores - row_top), axis=-1, keepdims=True))
        soft_probs = jnp.exp(scores - log_total).astype(jnp.bfloat16)
        context = jnp.einsum(
            "gqk,gkd->gqd", soft_probs, value_group, preferred_element_type=jnp.float32
        ).astype(jnp.bfloat16)
        return (context, log_total[..., 0])

    context, log_total = lax.map(forward_group, (query_groups, layout_groups))
    return (context.reshape(seq_len, head_width), log_total.reshape(seq_len))


def block_backward(queries, key_rows, values, layout, context, log_total, grad_rows):
    seq_len, head_width = queries.shape
    block_count, key_count = layout.shape
    block_len = seq_len // block_count
    row_group = group_size(block_count, block_len)
    group_count = block_count // row_group
    score_scale = 1.0 / math.sqrt(head_width)
    key_blocks = key_rows.reshape(block_count, block_len, head_width)
    value_blocks = values.reshape(block_count, block_len, head_width)
    query_groups = queries.reshape(group_count, row_group, block_len, head_width)
    layout_groups = layout.reshape(group_count, row_group, key_count)
    context_groups = context.reshape(group_count, row_group, block_len, head_width)
    total_groups = log_total.reshape(group_count, row_group, block_len)
    grad_groups = grad_rows.reshape(group_count, row_group, block_len, head_width)

    def backward_group(running, packed):
        key_acc, value_acc = running
        query_group, layout_group, context_group, total_group, grad_group = packed
        key_group = key_blocks[layout_group].reshape(row_group, key_count * block_len, head_width)
        value_group = value_blocks[layout_group].reshape(
            row_group, key_count * block_len, head_width
        )
        scores = (
            jnp.einsum("gqd,gkd->gqk", query_group, key_group, preferred_element_type=jnp.float32)
            * score_scale
        )
        exact_probs = jnp.exp(scores - total_group[..., None])
        soft_probs = exact_probs.astype(jnp.bfloat16)
        grad_probs = jnp.einsum(
            "gqd,gkd->gqk", grad_group, value_group, preferred_element_type=jnp.float32
        )
        row_delta = jnp.sum(
            grad_group.astype(jnp.float32) * context_group.astype(jnp.float32),
            axis=-1,
            keepdims=True,
        )
        grad_scores = (exact_probs * (grad_probs - row_delta)).astype(jnp.bfloat16)
        grad_query = (
            jnp.einsum("gqk,gkd->gqd", grad_scores, key_group, preferred_element_type=jnp.float32)
            * score_scale
        ).astype(jnp.bfloat16)
        key_part = (
            jnp.einsum("gqk,gqd->gkd", grad_scores, query_group, preferred_element_type=jnp.float32)
            * score_scale
        )
        value_part = jnp.einsum(
            "gqk,gqd->gkd", soft_probs, grad_group, preferred_element_type=jnp.float32
        )
        flat_index = layout_group.reshape(-1)
        key_acc = key_acc.at[flat_index].add(
            key_part.reshape(row_group * key_count, block_len, head_width)
        )
        value_acc = value_acc.at[flat_index].add(
            value_part.reshape(row_group * key_count, block_len, head_width)
        )
        return ((key_acc, value_acc), grad_query)

    initial = jnp.zeros((block_count, block_len, head_width), jnp.float32)
    (key_acc, value_acc), grad_query = lax.scan(
        backward_group,
        (initial, initial),
        (query_groups, layout_groups, context_groups, total_groups, grad_groups),
    )
    grad_key = key_acc.reshape(seq_len, head_width).astype(jnp.bfloat16)
    grad_value = value_acc.reshape(seq_len, head_width).astype(jnp.bfloat16)
    return (grad_query.reshape(seq_len, head_width), grad_key, grad_value)


def weight_term(source_rows, masked_grad):
    return lax.dot_general(
        source_rows, masked_grad, (((0,), (0,)), ((), ())), preferred_element_type=jnp.float32
    )


def on_device(projected, out_weight, upstream, peak_mask, block_layout):
    tokens_here = projected.shape[1]
    triple_width = projected.shape[2]
    inner_width = triple_width // 3
    head_count = inner_width // HS
    model_width = out_weight.shape[1]
    local_rows = projected[0].reshape(tokens_here, 3, head_count, HS)
    head_rows = lax.all_to_all(local_rows, "seq", split_axis=2, concat_axis=0, tiled=True)
    head_index = 0
    context, log_total = block_forward(
        head_rows[:, 0, head_index],
        head_rows[:, 1, head_index],
        head_rows[:, 2, head_index],
        block_layout[head_index],
    )
    contexts = [context]
    totals = [log_total]
    context_heads = jnp.stack(contexts, axis=1)
    token_context = lax.all_to_all(
        context_heads, "seq", split_axis=0, concat_axis=1, tiled=True
    ).reshape(tokens_here, inner_width)
    masked_grad = upstream[0] * peak_mask[0][:, None].astype(jnp.bfloat16)
    full_weight = lax.all_gather(out_weight, ("dp", "seq"), axis=0, tiled=True)
    attended = jnp.dot(token_context, full_weight, preferred_element_type=jnp.float32)
    grad_context = lax.dot_general(
        masked_grad, full_weight, (((1,), (1,)), ((), ())), preferred_element_type=jnp.float32
    )
    attended = attended.astype(jnp.bfloat16)
    grad_context = grad_context.astype(jnp.bfloat16)
    grad_heads = lax.all_to_all(
        grad_context.reshape(tokens_here, head_count, HS),
        "seq",
        split_axis=1,
        concat_axis=0,
        tiled=True,
    )
    head_index = 0
    grad_query, grad_key, grad_value = block_backward(
        head_rows[:, 0, head_index],
        head_rows[:, 1, head_index],
        head_rows[:, 2, head_index],
        block_layout[head_index],
        contexts[head_index],
        totals[head_index],
        grad_heads[:, head_index],
    )
    pieces = [jnp.stack([grad_query, grad_key, grad_value], axis=1)]
    grad_split = jnp.stack(pieces, axis=2)
    token_grads = lax.all_to_all(
        grad_split, "seq", split_axis=0, concat_axis=2, tiled=True
    ).reshape(1, tokens_here, triple_width)
    weight_grad = lax.psum_scatter(
        weight_term(token_context, masked_grad), ("dp", "seq"), scatter_dimension=0, tiled=True
    )
    return (attended.reshape(1, tokens_here, model_width), token_grads, weight_grad)


def solution(mesh):
    in_specs = (
        P("dp", "seq", None),
        P(("dp", "seq"), None),
        P("dp", "seq", None),
        P("dp", "seq"),
        P("seq", None, None),
    )
    out_specs = (P("dp", "seq", None), P("dp", "seq", None), P(("dp", "seq"), None))
    return jax.shard_map(
        on_device, mesh=mesh, in_specs=in_specs, out_specs=out_specs, check_vma=False
    )
```

profile of v0, /device:TPU:0, one launch (start us, length us, event | category | flops | bytes accessed | tf_op | source)
XLA Modules:
  0.0 1496.6 jit_solution(886526390044861542)
XLA Ops:
  10.3 9.9 all-to-all-start
  21.1 38.7 %all-to-all-done = bf16[128,3,32,64]{0,3,1,2:T(8,128)(2,1)S(1)} async-done(((bf16[128,3,32,64]{0,3,1,2:T(8,128)(2,1)}), bf16[128,3,32,64]{0,3,1,2:T(8,128)(2,1)S(1)}, u32[]{:S(2)}, u32[]{:S(2)}) %all-to-all-start) | async-done | bytes 1572896 | tf_op jit(solution)/shard_map/all_to_all | solution.py:130
  63.5 47.7 %while.26 = (s32[]{:T(128)}, bf16[8,4,128,64]{2,3,1,0:T(8,128)(2,1)S(1)}, f32[8,4,128]{2,1,0:T(4,128)S(1)}, bf16[8,4,128,64]{2,3,1,0:T(8,128)(2,1)S(1)}, s32[8,4...) while((s32[]{:T(128)}, ...), condition=%wide.region_3.4_spmd, body=%wide.region_0.3_spmd.sunk | while | flops 138445408 | bytes 10638317 | solution.py:45
  112.5 5.8 reshape.259
  118.9 23.4 %reduce = bf16[4096,64]{1,0:T(8,128)(2,1)} reduce(bf16[4096,1,64]{2,1,0:T(2,128)(2,1)S(1)} %reshape.259, bf16[]{:T(256)} %broadcast.112), dimensions={1}, to_apply=%reshape.259.reduce_sub_computation | reduce | bytes 1048578 | tf_op jit(solution)/shard_map/stack;reshape | solution.py:140
  145.4 5.7 all-to-all-start.1
  151.3 16.4 %all-to-all-done.1 = bf16[32,2,4096]{2,1,0:T(2,128)(2,1)S(1)} async-done(((bf16[32,2,4096]{2,1,0:T(2,128)(2,1)}), bf16[32,2,4096]{2,1,0:T(2,128)(2,1)S(1)}, u32[]{:S(2)}, u32[]{:S(2)}) %all-to-all-start.1) | async-done | bytes 524320 | tf_op jit(solution)/shard_map/all_to_all | solution.py:141
  174.8 8.1 fusion.33
  183.0 6.3 convolution_convert_fusion.1
  195.0 19.1 %all-to-all-done.2 = bf16[128,32,64]{0,2,1:T(8,128)(2,1)} async-done(((bf16[128,32,64]{0,2,1:T(8,128)(2,1)}), bf16[128,32,64]{0,2,1:T(8,128)(2,1)}, u32[]{:S(2)}, u32[]{:S(2)}) %all-to-all-start.2) | async-done | bytes 524320 | tf_op jit(solution)/shard_map/all_to_all | solution.py:152
  216.4 241.8 %while.27 = (s32[]{:T(128)}, f32[32,128,64]{1,2,0:T(8,128)}, f32[32,128,64]{1,2,0:T(8,128)}, bf16[8,4,128,64]{2,1,0,3:T(4,128)(2,1)}, s32[8,4,8]{2,1,0:T(4,128)S...) while((s32[]{:T(128)}, f32[32,128,64]{1,2,0:T(8,128)}, ...), condition=%wide.region_8.9_spmd, body=%wide.region_4.8_spmd.sunk | while | flops 340722368 | bytes 51988548 | solution.py:107
  232.5 4.8 scatter_fusion
  240.5 4.9 scatter_fusion.1
  262.7 4.8 scatter_fusion
  270.7 4.9 scatter_fusion.1
  292.9 4.8 scatter_fusion
  300.9 4.9 scatter_fusion.1
  323.2 4.8 scatter_fusion
  331.1 4.9 scatter_fusion.1
  353.4 4.8 scatter_fusion
  361.4 4.9 scatter_fusion.1
  383.6 4.8 scatter_fusion
  391.6 4.9 scatter_fusion.1
  413.8 4.8 scatter_fusion
  421.8 4.9 scatter_fusion.1
  444.0 4.8 scatter_fusion
  452.0 4.9 scatter_fusion.1
  466.5 7.2 reshape.262
  477.9 5.5 fusion.32
  483.3 34.7 %all-to-all-done.3 = bf16[32,2,12288]{2,1,0:T(2,128)(2,1)S(1)} async-done(((bf16[32,2,12288]{2,1,0:T(2,128)(2,1)}), bf16[32,2,12288]{2,1,0:T(2,128)(2,1)S(1)}, u32[]{:S(2)}, u32[]{:S(2)}) %all-to-all-start.3) | async-done | bytes 1572896 | tf_op jit(solution)/shard_map/all_to_all | solution.py:171
  522.8 5.8 copy.103
  530.2 959.6 %reduce-scatter.2.cloned.1.call-done = f32[8,2048]{1,0:T(8,128)} async-done(((f32[2048,2048]{1,0:T(8,128)}), f32[8,2048]{1,0:T(8,128)}) %reduce-scatter.2.cloned.1.call-update) | async-done | bytes 65552 | tf_op jit(solution)/shard_map/reduce_scatter | solution.py:174
  (393 shorter events, 257.5 us)
Async XLA Ops:
  10.3 10.6 copy-start.12
  10.3 49.4 %all-to-all-start = ((bf16[128,3,32,64]{0,3,1,2:T(8,128)(2,1)}), bf16[128,3,32,64]{0,3,1,2:T(8,128)(2,1)S(1)}, u32[]{:S(2)}, u32[]{:S(2)}) async-start(bf16[128,3,32,64]{0,3,1,2:T(8,128)(2,1)} %copy.75), calls=%async_computation | async-start | bytes 3145728 | tf_op jit(solution)/shard_map/all_to_all | solution.py:130
  20.2 162.7 %all-gather.2.cloned.1.call-start = ((), (), s32[]{:S(2)}) async-start(), calls=%async_computation.5 | async-start | bytes 8421376 | tf_op jit(solution)/shard_map/all_gather | solution.py:145
  111.2 7.2 copy-start.10
  142.3 9.1 copy-start.13
  145.4 22.4 %all-to-all-start.1 = ((bf16[32,2,4096]{2,1,0:T(2,128)(2,1)}), bf16[32,2,4096]{2,1,0:T(2,128)(2,1)S(1)}, u32[]{:S(2)}, u32[]{:S(2)}) async-start(bf16[32,2,4096]{2,1,0:T(2,128)(2,1)} %reshape.260), calls=%async_computation.1 | async-start | bytes 1048576 | tf_op jit(solution)/shard_map/all_to_all | solution.py:141
  151.1 1338.7 %reduce-scatter.2.cloned.1.call-start = ((), (), s32[]{:S(2)}) async-start(), calls=%async_computation.6 | async-start | bytes 16842752 | tf_op jit(solution)/shard_map/reduce_scatter | solution.py:174
  169.0 5.8 copy-start.9
  190.3 23.7 %all-to-all-start.2 = ((bf16[128,32,64]{0,2,1:T(8,128)(2,1)}), bf16[128,32,64]{0,2,1:T(8,128)(2,1)}, u32[]{:S(2)}, u32[]{:S(2)}) async-start(bf16[128,32,64]{0,2,1:T(8,128)(2,1)} %bitcast.24), calls=%async_computation.2 | async-start | bytes 1048576 | tf_op jit(solution)/shard_map/all_to_all | solution.py:152
  240.4 4.9 copy-start.1
  240.4 4.9 copy-start.3
  249.4 4.3 copy-start
  270.6 4.9 copy-start.1
  270.7 4.9 copy-start.3
  279.6 4.3 copy-start
  300.9 4.9 copy-start.1
  300.9 4.9 copy-start.3
  309.9 4.3 copy-start
  331.1 4.9 copy-start.1
  331.1 4.9 copy-start.3
  340.1 4.3 copy-start
  361.3 4.9 copy-start.1
  361.3 4.9 copy-start.3
  391.6 4.9 copy-start.1
  391.6 4.9 copy-start.3
  400.5 4.3 copy-start
  421.8 4.9 copy-start.1
  421.8 4.9 copy-start.3
  430.7 4.3 copy-start
  452.0 4.9 copy-start.1
  452.0 4.9 copy-start.3
  473.7 44.3 %all-to-all-start.3 = ((bf16[32,2,12288]{2,1,0:T(2,128)(2,1)}), bf16[32,2,12288]{2,1,0:T(2,128)(2,1)S(1)}, u32[]{:S(2)}, u32[]{:S(2)}) async-start(bf16[32,2,12288]{2,1,0:T(2,128)(2,1)} %reshape.262), calls=%async_computation.3 | async-start | bytes 3145728 | tf_op jit(solution)/shard_map/all_to_all | solution.py:171
  (30 other events, 41.2 us)
Sparse Core Ops, SparseCore 0:
  24.9 121.2 all-gather.1
  183.1 1306.6 reduce-scatter.1
where the time goes:
time: 1500 us
  waiting for transfers between devices  1070 us (71%)
  local copies, waits for them, and re-layouts  190 us (13%)
  other arithmetic  114 us (8%)
  matrix products  82.8 us (6%)
  starting transfers between devices  24.6 us (2%)
    reduce_scatter x1, waiting for transfers between devices, on_device(): lax.psum_scatter(weight_term(token_context, masked_grad), ('dp', 'seq'),...  960 us
    scatter-add x8, other arithmetic, backward_group(): value_acc.at[flat_index]  39 us
    all_to_all x1, waiting for transfers between devices, on_device(): lax.all_to_all(local_rows, 'seq', split_axis=2, concat_axis=0, tiled=True)  38.7 us
    scatter-add x8, other arithmetic, backward_group(): key_acc.at[flat_index]  38.3 us
    all_to_all x1, waiting for transfers between devices, on_device(): lax.all_to_all(grad_split, 'seq', split_axis=0, concat_axis=2, tiled=True)  34.7 us
  transfers between devices with their start and end apart: 6, of which 5 were waited for; matrix products, arithmetic and copies ran while one was open for 25% of the time, Pallas kernels for 0%

commit v1 on v0

v1 whole, which is shorter than its diff:
```python
import jax
import jax.numpy as jnp
from jax import lax
from jax.experimental import pallas as pl
from jax.experimental.pallas import tpu as pltpu
from jax.sharding import PartitionSpec as P

HS = 64
SCALE = 0.125


def attention_kernel(layout, qkv, grad, out, kvn, acc, probs, scores):
    blocks, _, head, length = qkv.shape
    picks = layout.shape[1]
    pair = 2 * head

    def prepare(b, carry):
        kvn[b] = qkv[b, 1:3].reshape(pair, length).T
        acc[b] = jnp.zeros((length, pair), jnp.float32)
        return carry

    lax.fori_loop(0, blocks, prepare, 0)
    low = lax.broadcasted_iota(jnp.int32, (length, pair), 1) < head

    def row_block(r, carry):
        q = qkv[r, 0] * jnp.bfloat16(SCALE)
        g = grad[r]
        none = jnp.zeros_like(q)
        turned = jnp.concatenate([q, g], 0).T
        into_scores = jnp.concatenate(
            [jnp.concatenate([q, none], 1), jnp.concatenate([none, g], 1)], 0
        )
        into_keys = jnp.concatenate(
            [jnp.where(low, turned, 0), jnp.where(low, 0, turned)], 0
        )
        at = [layout[r, j] for j in range(picks)]
        top = None
        for j in range(picks):
            both = jnp.dot(kvn[at[j]], into_scores, preferred_element_type=jnp.float32)
            scores[j] = both
            part = jnp.max(both[:, :length].reshape(length // 8, 8, length), axis=0)
            top = part if top is None else jnp.maximum(top, part)
        top = jnp.max(top, axis=0, keepdims=True)
        total = jnp.zeros((8, length), jnp.float32)
        delta = jnp.zeros((8, length), jnp.float32)
        for j in range(picks):
            e = jnp.exp(scores[j, :, :length] - top)
            scores[j, :, :length] = e
            total += jnp.sum(e.reshape(length // 8, 8, length), axis=0)
            delta += jnp.sum((e * scores[j, :, length:]).reshape(length // 8, 8, length), axis=0)
        inverse = 1.0 / jnp.sum(total, axis=0, keepdims=True)
        delta = jnp.sum(delta, axis=0, keepdims=True) * inverse
        for j in range(picks):
            p = scores[j, :, :length] * inverse
            d = p * (scores[j, :, length:] - delta)
            rows = pl.ds(j * length, length)
            probs[rows, :length] = d.astype(jnp.bfloat16)
            probs[rows, length:] = p.astype(jnp.bfloat16)
        kvt = jnp.concatenate([qkv[at[j], 1:3].reshape(pair, length) for j in range(picks)], 1)
        both = jnp.dot(kvt, probs[...], preferred_element_type=jnp.float32)
        out[r, 0] = both[head:, length:].astype(jnp.bfloat16)
        out[r, 1] = (both[:head, :length] * SCALE).astype(jnp.bfloat16)
        for j in range(picks):
            acc[at[j]] += jnp.dot(
                probs[pl.ds(j * length, length), :], into_keys, preferred_element_type=jnp.float32
            )
        return carry

    lax.fori_loop(0, blocks, row_block, 0)

    def finish(b, carry):
        out[b, 2:4] = acc[b].T.astype(jnp.bfloat16).reshape(2, head, length)
        return carry

    lax.fori_loop(0, blocks, finish, 0)


def attention(layout, qkv, grad):
    blocks, _, head, length = qkv.shape
    picks = layout.shape[1]
    keys = picks * length
    vmem = pl.BlockSpec(memory_space=pltpu.VMEM)
    return pl.pallas_call(
        attention_kernel,
        name="attention",
        out_shape=jax.ShapeDtypeStruct((blocks, 4, head, length), jnp.bfloat16),
        in_specs=[pl.BlockSpec(memory_space=pltpu.SMEM), vmem, vmem],
        out_specs=vmem,
        scratch_shapes=[
            pltpu.VMEM((blocks, length, 2 * head), jnp.bfloat16),
            pltpu.VMEM((blocks, length, 2 * head), jnp.float32),
            pltpu.VMEM((keys, 2 * length), jnp.bfloat16),
            pltpu.VMEM((picks, length, 2 * length), jnp.float32),
        ],
        cost_estimate=pl.CostEstimate(
            flops=12 * blocks * length * keys * head,
            bytes_accessed=16 * blocks * length * head,
            transcendentals=blocks * length * keys,
        ),
        compiler_params=pltpu.CompilerParams(vmem_limit_bytes=32 << 20),
    )(layout, qkv, grad)


def on_device(projected, out_weight, upstream, peak_mask, block_layout):
    tokens = projected.shape[1]
    inner = projected.shape[2] // 3
    heads = inner // HS
    model = out_weight.shape[1]
    dp = lax.axis_size("dp")
    seq = lax.axis_size("seq")

    turned = projected[0].T.reshape(3, heads, HS, tokens).transpose(1, 0, 2, 3)
    qkv = lax.all_to_all(turned, "seq", split_axis=0, concat_axis=0, tiled=True)
    full_weight = lax.all_gather(out_weight, ("dp", "seq"), axis=0, tiled=True)
    masked_grad = upstream[0] * peak_mask[0][:, None].astype(jnp.bfloat16)
    run_grads = lax.all_gather(masked_grad, "dp", axis=0, tiled=True)
    grad_context = lax.dot_general(
        full_weight, masked_grad, (((1,), (1,)), ((), ())), preferred_element_type=jnp.float32
    ).astype(jnp.bfloat16)
    grad_heads = lax.all_to_all(
        grad_context.reshape(heads, HS, tokens), "seq", split_axis=0, concat_axis=0, tiled=True
    )
    results = attention(block_layout[0], qkv, grad_heads)
    back = lax.all_to_all(results, "seq", split_axis=0, concat_axis=0, tiled=True)
    context = back[:, 0].reshape(inner, tokens)
    projected_grad = back[:, 1:].transpose(3, 1, 0, 2).reshape(1, tokens, 3 * inner)
    attended = lax.dot_general(
        context, full_weight, (((0,), (0,)), ((), ())), preferred_element_type=jnp.float32
    ).astype(jnp.bfloat16)
    run_context = lax.all_to_all(
        context.reshape(dp, inner // dp, tokens), "dp", split_axis=0, concat_axis=0, tiled=True
    )
    run_context = run_context.transpose(1, 0, 2).reshape(inner // dp, dp * tokens)
    partial = jnp.dot(run_context, run_grads, preferred_element_type=jnp.float32)
    pieces = lax.all_to_all(
        partial.astype(jnp.bfloat16).reshape(seq, inner // (dp * seq), model),
        "seq",
        split_axis=0,
        concat_axis=0,
        tiled=True,
    )
    weight_grad = jnp.sum(pieces.astype(jnp.float32), axis=0)
    return (attended.reshape(1, tokens, model), projected_grad, weight_grad)


def solution(mesh):
    in_specs = (
        P("dp", "seq", None),
        P(("dp", "seq"), None),
        P("dp", "seq", None),
        P("dp", "seq"),
        P("seq", None, None),
    )
    out_specs = (P("dp", "seq", None), P("dp", "seq", None), P(("dp", "seq"), None))
    return jax.shard_map(
        on_device, mesh=mesh, in_specs=in_specs, out_specs=out_specs, check_vma=False
    )
```

time: 1500 us -> 322 us (0.21)
  the two profiles are of different devices: /device:TPU:0 before, /device:TPU:1 now
where the time goes in v1:
time: 322 us; the launch traced here: 319 us
  waiting for transfers between devices  158 us (49%)
  blocking collectives  52.9 us (16%)
  Pallas kernels  36.8 us (11%)
  starting transfers between devices  30.6 us (10%)
  matrix products  16.4 us (5%)
  between operations  14.2 us (4%)
  local copies, waits for them, and re-layouts  7.19 us (2%)
    all_gather x1, waiting for transfers between devices, on_device(): full_weight = lax.all_gather(out_weight, ('dp', 'seq'), axis=0, tiled=True)  113 us
    all_to_all x1, blocking collectives, on_device(): lax.all_to_all(results, 'seq', split_axis=0, concat_axis=0, tiled=True)  52.9 us
    pallas_call x1, Pallas kernels, attention(): pl.pallas_call(attention_kernel, name='attention', out_shape=jax.ShapeDty...  36.8 us
    all_to_all x1, waiting for transfers between devices, on_device(): lax.all_to_all(partial.astype(jnp.bfloat16).reshape(seq, inner // (dp * s...  18.7 us
    all_to_all x1, waiting for transfers between devices, on_device(): lax.all_to_all(grad_context.reshape(heads, HS, tokens), 'seq', split_axis...  16.5 us
    all_to_all x1, starting transfers between devices, on_device(): qkv = lax.all_to_all(turned, 'seq', split_axis=0, concat_axis=0, tiled=True)  12.2 us
    all_to_all x1, waiting for transfers between devices, on_device(): lax.all_to_all(context.reshape(dp, inner // dp, tokens), 'dp', split_axis...  9.5 us
    all_to_all x1, starting transfers between devices, on_device(): lax.all_to_all(context.reshape(dp, inner // dp, tokens), 'dp', split_axis...  6.76 us
  transfers between devices with their start and end apart: 6, of which 4 were waited for; matrix products, arithmetic and copies ran while one was open for 6% of the time, Pallas kernels for 12%

profile of v1, /device:TPU:1, one launch (start us, length us, event | category | flops | bytes accessed | tf_op | source)
XLA Modules:
  0.0 319.3 jit_solution(1709739117782012459)
XLA Ops:
  7.2 0.0 all-gather.3.cloned.1.call-start
  7.2 0.7 all-gather.3.cloned.1.call-update
  7.9 1.9 copy.11
  9.8 1.3 copy.18
  11.1 12.2 %all-to-all-start = ((bf16[32,3,64,128]{3,2,1,0:T(8,128)(2,1)}), bf16[32,3,64,128]{3,2,1,0:T(8,128)(2,1)S(1)}, u32[]{:S(2)}, u32[]{:S(2)}) async-start(bf16[32,3,64,128]{3,2,1,0:T(8,128)(2,1)} %bitcast.33), calls=%async_computation | async-start | bytes 3145728 | tf_op jit(solution)/shard_map/all_to_all | solution.py:113
  23.3 0.0 all-gather.5.cloned.1.call-start
  23.3 0.0 copy-done.2
  23.3 0.0 copy-done
  23.3 0.9 bitcast_multiply_fusion
  24.2 0.0 all-gather.5.cloned.1.call-update
  24.3 113.0 %all-gather.3.cloned.1.call-done = bf16[2048,2048]{1,0:T(8,128)(2,1)} async-done(((bf16[8,2048]{1,0:T(8,128)(2,1)}), bf16[2048,2048]{1,0:T(8,128)(2,1)}) %all-gather.3.cloned.1.call-update) | async-done | bytes 8388624 | tf_op jit(solution)/shard_map/all_gather | solution.py:114
  137.3 6.4 %fusion.1 = bf16[2048,128]{0,1:T(8,128)(2,1)S(1)} fusion(bf16[128,2048]{1,0:T(8,128)(2,1)} %bitcast_multiply_fusion, bf16[2048,2048]{1,0:T(8,128)(2,1)} %all-gather.3.cloned.1.call-done), kind=kOutput, calls=%fused_computation.4 | convolution fusion | flops 1074003968 | bytes 9437184 | tf_op jit(solution)/shard_map/dot_general | solution.py:117
  143.7 0.0 copy-start.1
  143.7 1.0 copy.13
  144.8 0.0 all-to-all-done.qkv
  144.8 6.2 %all-to-all-start.1 = ((bf16[32,64,128]{2,1,0:T(8,128)(2,1)}), bf16[32,64,128]{2,1,0:T(8,128)(2,1)S(1)}, u32[]{:S(2)}, u32[]{:S(2)}) async-start(bf16[32,64,128]{2,1,0:T(8,128)(2,1)} %bitcast.8), calls=%async_computation.1 | async-start | bytes 1048576 | tf_op jit(solution)/shard_map/all_to_all | solution.py:120
  151.0 0.0 copy-done.1
  151.0 0.1 copy.10
  151.0 16.5 %all-to-all-done.1.grad = bf16[32,64,128]{2,1,0:T(8,128)(2,1)S(1)} async-done(((bf16[32,64,128]{2,1,0:T(8,128)(2,1)}), bf16[32,64,128]{2,1,0:T(8,128)(2,1)S(1)}, u32[]{:S(2)}, u32[]{:S(2)}) %all-to-all-start.1) | async-done | bytes 524320 | tf_op jit(solution)/shard_map/all_to_all | solution.py:120
  167.6 36.8 %attention.1 = bf16[32,4,64,128]{3,2,1,0:T(8,128)(2,1)S(1)} custom-call(s32[32,8]{1,0:T(8,128)S(1)} %bitcast.34, bf16[32,3,64,128]{3,2,1,0:T(8,128)(2,1)S(1)} %all-to-all-done.qkv, bf16[32,64,128]{2,1,0:T(8,128)(2,1)S(1)} %all-to-all-done.1.grad), custom_call_target="tpu_custom_call" | custom-call | flops 3221225472 | bytes 4194304 | tf_op jit(solution)/shard_map/attention/pallas_call | solution.py:83
  204.4 52.9 %all_to_all.25 = bf16[32,4,64,128]{3,2,1,0:T(8,128)(2,1)S(1)} all-to-all(bf16[32,4,64,128]{3,2,1,0:T(8,128)(2,1)S(1)} %attention.1), channel_id=1, replica_groups=mesh['dp'=8,'seq'=32] {'seq'}, dimensions={0} | all-to-all | bytes 4194304 | tf_op jit(solution)/shard_map/all_to_all | solution.py:124
  257.3 1.0 copy.15
  258.3 6.8 %all-to-all-start.3 = ((bf16[8,256,128]{1,2,0:T(8,128)(2,1)}), bf16[8,256,128]{1,2,0:T(8,128)(2,1)S(1)}, u32[]{:S(2)}, u32[]{:S(2)}) async-start(bf16[8,256,128]{1,2,0:T(8,128)(2,1)} %copy.15), calls=%async_computation.3 | async-start | bytes 1048576 | tf_op jit(solution)/shard_map/all_to_all | solution.py:130
  265.0 9.5 %all-to-all-done.3 = bf16[8,256,128]{1,2,0:T(8,128)(2,1)S(1)} async-done(((bf16[8,256,128]{1,2,0:T(8,128)(2,1)}), bf16[8,256,128]{1,2,0:T(8,128)(2,1)S(1)}, u32[]{:S(2)}, u32[]{:S(2)}) %all-to-all-start.3) | async-done | bytes 524320 | tf_op jit(solution)/shard_map/all_to_all | solution.py:130
  274.5 4.5 %fusion = bf16[32,8,2048]{2,1,0:T(8,128)(2,1)} fusion(bf16[256,1024]{0,1:T(8,128)(2,1)S(1)} %bitcast.39, bf16[1024,2048]{1,0:T(8,128)(2,1)} %all-gather.5.cloned.1.call-done), kind=kOutput, calls=%fused_computation.1 | convolution fusion | flops 1074266112 | bytes 5767168 | tf_op jit(solution)/shard_map/dot_general | solution.py:134
  279.1 5.4 %all-to-all-start.4 = ((bf16[32,8,2048]{2,1,0:T(8,128)(2,1)}), bf16[32,8,2048]{2,1,0:T(8,128)(2,1)}, u32[]{:S(2)}, u32[]{:S(2)}) async-start(bf16[32,8,2048]{2,1,0:T(8,128)(2,1)} %fusion), calls=%async_computation.4 | async-start | bytes 2097152 | tf_op jit(solution)/shard_map/all_to_all | solution.py:135
  284.5 0.2 slice_bitcast_fusion
  284.7 0.1 copy.14
  284.8 1.6 copy.16
  286.4 5.5 %fusion.2 = bf16[1,128,2048]{2,1,0:T(8,128)(2,1)} fusion(bf16[2048,128]{1,0:T(8,128)(2,1)S(1)} %bitcast.36, bf16[2048,2048]{1,0:T(8,128)(2,1)} %all-gather.3.cloned.1.call-done), kind=kOutput, calls=%fused_computation.5 | convolution fusion | flops 1074003968 | bytes 9437184 | tf_op jit(solution)/shard_map/dot_general | solution.py:127
  291.8 18.7 %all-to-all-done.4 = bf16[32,8,2048]{2,1,0:T(8,128)(2,1)} async-done(((bf16[32,8,2048]{2,1,0:T(8,128)(2,1)}), bf16[32,8,2048]{2,1,0:T(8,128)(2,1)}, u32[]{:S(2)}, u32[]{:S(2)}) %all-to-all-start.4) | async-done | bytes 1048608 | tf_op jit(solution)/shard_map/all_to_all | solution.py:135
  310.5 2.0 convert_reduce_fusion
  (5 shorter events, 0.0 us)
Async XLA Ops:
  7.2 130.1 %all-gather.3.cloned.1.call-start = ((), (), s32[]{:S(2)}) async-start(), calls=%async_computation.5 | async-start | bytes 8421376 | tf_op jit(solution)/shard_map/all_gather | solution.py:114
  11.1 12.2 %copy-start.2 = (s32[1,128]{1,0:T(1,128)S(1)}, s32[1,128]{1,0:T(1,128)}, u32[]{:S(2)}) copy-start(s32[1,128]{1,0:T(1,128)} %param.8) | copy-start | bytes 1540
  11.1 12.3 %copy-start = (bf16[1,128,2048]{2,1,0:T(8,128)(2,1)S(1)}, bf16[1,128,2048]{2,1,0:T(8,128)(2,1)}, u32[]{:S(2)}) copy-start(bf16[1,128,2048]{2,1,0:T(8,128)(2,1)} %param.7) | copy-start | bytes 1572868
  11.1 133.7 %all-to-all-start = ((bf16[32,3,64,128]{3,2,1,0:T(8,128)(2,1)}), bf16[32,3,64,128]{3,2,1,0:T(8,128)(2,1)S(1)}, u32[]{:S(2)}, u32[]{:S(2)}) async-start(bf16[32,3,64,128]{3,2,1,0:T(8,128)(2,1)} %bitcast.33), calls=%async_computation | async-start | bytes 3145728 | tf_op jit(solution)/shard_map/all_to_all | solution.py:113
  23.3 241.8 %all-gather.5.cloned.1.call-start = ((), (), s32[]{:S(2)}) async-start(), calls=%async_computation.6 | async-start | bytes 4718592 | tf_op jit(solution)/shard_map/all_gather | solution.py:116
  143.7 7.2 %copy-start.1 = (s32[1,32,8]{1,2,0:T(8,128)S(1)}, s32[1,32,8]{1,2,0:T(8,128)}, u32[]{:S(2)}) copy-start(s32[1,32,8]{1,2,0:T(8,128)} %param.9) | copy-start | bytes 3076
  144.8 22.8 %all-to-all-start.1 = ((bf16[32,64,128]{2,1,0:T(8,128)(2,1)}), bf16[32,64,128]{2,1,0:T(8,128)(2,1)S(1)}, u32[]{:S(2)}, u32[]{:S(2)}) async-start(bf16[32,64,128]{2,1,0:T(8,128)(2,1)} %bitcast.8), calls=%async_computation.1 | async-start | bytes 1048576 | tf_op jit(solution)/shard_map/all_to_all | solution.py:120
  258.3 16.3 %all-to-all-start.3 = ((bf16[8,256,128]{1,2,0:T(8,128)(2,1)}), bf16[8,256,128]{1,2,0:T(8,128)(2,1)S(1)}, u32[]{:S(2)}, u32[]{:S(2)}) async-start(bf16[8,256,128]{1,2,0:T(8,128)(2,1)} %copy.15), calls=%async_computation.3 | async-start | bytes 1048576 | tf_op jit(solution)/shard_map/all_to_all | solution.py:130
  279.1 31.4 %all-to-all-start.4 = ((bf16[32,8,2048]{2,1,0:T(8,128)(2,1)}), bf16[32,8,2048]{2,1,0:T(8,128)(2,1)}, u32[]{:S(2)}, u32[]{:S(2)}) async-start(bf16[32,8,2048]{2,1,0:T(8,128)(2,1)} %fusion), calls=%async_computation.4 | async-start | bytes 2097152 | tf_op jit(solution)/shard_map/all_to_all | solution.py:135
Sparse Core Ops, SparseCore 0:
  11.8 125.3 all-gather.2
  139.7 31.3 all-gather.4

commit v2 on v1

--- a/solution.py
+++ b/solution.py
@@ -111,12 +111,15 @@
 
     turned = projected[0].T.reshape(3, heads, HS, tokens).transpose(1, 0, 2, 3)
     qkv = lax.all_to_all(turned, "seq", split_axis=0, concat_axis=0, tiled=True)
-    full_weight = lax.all_gather(out_weight, ("dp", "seq"), axis=0, tiled=True)
+    run_weight = lax.all_gather(out_weight, "seq", axis=0, tiled=True)
     masked_grad = upstream[0] * peak_mask[0][:, None].astype(jnp.bfloat16)
     run_grads = lax.all_gather(masked_grad, "dp", axis=0, tiled=True)
+    full_weight = lax.all_gather(run_weight, "dp", axis=0, tiled=True)
     grad_context = lax.dot_general(
-        full_weight, masked_grad, (((1,), (1,)), ((), ())), preferred_element_type=jnp.float32
+        run_weight, run_grads, (((1,), (1,)), ((), ())), preferred_element_type=jnp.float32
     ).astype(jnp.bfloat16)
+    grad_context = grad_context.reshape(inner // dp, dp, tokens).transpose(1, 0, 2)
+    grad_context = lax.all_to_all(grad_context, "dp", split_axis=0, concat_axis=0, tiled=True)
     grad_heads = lax.all_to_all(
         grad_context.reshape(heads, HS, tokens), "seq", split_axis=0, concat_axis=0, tiled=True
     )

time: 322 us -> 329 us (1.022)
  blocking collectives: 52.9 us -> 91 us
  starting transfers between devices: 30.6 us -> 15.9 us
  waiting for transfers between devices: 158 us -> 147 us
    all_to_all x0 -> x2, blocking collectives: none -> 37.4 us  [the longest x1 21.7 us: on_device(): lax.all_to_all(grad_context, 'dp', split_axis=0, concat_axis=0, tiled=True)]
    all_gather x1 -> x2, waiting for transfers between devices: 113 us -> 75.6 us  [the longest x1 75.6 us: on_device(): run_weight = lax.all_gather(out_weight, 'seq', axis=0, tiled=True)]
    all_gather x1, waiting for transfers between devices: 0.01 us -> 31.5 us  [on_device(): run_grads = lax.all_gather(masked_grad, 'dp', axis=0, tiled=True)]
    all_to_all x1 -> x0, waiting for transfers between devices: 9.5 us -> none  [on_device(): lax.all_to_all(context.reshape(dp, inner // dp, tokens), 'dp', split_axis...]
    all_to_all x1 -> x0, starting transfers between devices: 6.76 us -> none  [on_device(): lax.all_to_all(context.reshape(dp, inner // dp, tokens), 'dp', split_axis...]
    all_to_all x1, starting transfers between devices: 12.2 us -> 5.83 us  [on_device(): qkv = lax.all_to_all(turned, 'seq', split_axis=0, concat_axis=0, tiled=True)]
    all_to_all x1, waiting for transfers between devices: 18.7 us -> 23.9 us  [on_device(): lax.all_to_all(partial.astype(jnp.bfloat16).reshape(seq, inner // (dp * s...]
  transfers between devices with their start and end apart: 6 -> 6, of which waited for: 4 -> 4; matrix products, arithmetic and copies ran while one was open for 6% -> 5% of each run, Pallas kernels for 12% -> 11%
where the time goes in v2:
time: 329 us; the launch traced here: 327 us
  waiting for transfers between devices  147 us (45%)
  blocking collectives  91 us (28%)
  Pallas kernels  36.8 us (11%)
  starting transfers between devices  15.9 us (5%)
  between operations  13.9 us (4%)
  matrix products  13.4 us (4%)
  local copies, waits for them, and re-layouts  4.65 us (1%)
  other arithmetic  4.61 us (1%)
    all_gather x1, waiting for transfers between devices, on_device(): run_weight = lax.all_gather(out_weight, 'seq', axis=0, tiled=True)  75.6 us
    all_to_all x1, blocking collectives, on_device(): lax.all_to_all(results, 'seq', split_axis=0, concat_axis=0, tiled=True)  53.6 us
    pallas_call x1, Pallas kernels, attention(): pl.pallas_call(attention_kernel, name='attention', out_shape=jax.ShapeDty...  36.8 us
    all_gather x1, waiting for transfers between devices, on_device(): run_grads = lax.all_gather(masked_grad, 'dp', axis=0, tiled=True)  31.5 us
    all_to_all x1, waiting for transfers between devices, on_device(): lax.all_to_all(partial.astype(jnp.bfloat16).reshape(seq, inner // (dp * s...  23.9 us
    all_to_all x1, blocking collectives, on_device(): lax.all_to_all(grad_context, 'dp', split_axis=0, concat_axis=0, tiled=True)  21.7 us
    all_to_all x1, blocking collectives, on_device(): lax.all_to_all(context.reshape(dp, inner // dp, tokens), 'dp', split_axis...  15.7 us
    all_to_all x1, waiting for transfers between devices, on_device(): lax.all_to_all(grad_context.reshape(heads, HS, tokens), 'seq', split_axis...  14.8 us
  transfers between devices with their start and end apart: 6, of which 4 were waited for; matrix products, arithmetic and copies ran while one was open for 5% of the time, Pallas kernels for 11%

profile of v2, /device:TPU:1, one launch (start us, length us, event | category | flops | bytes accessed | tf_op | source)
XLA Modules:
  0.0 326.8 jit_solution(17999716985593097223)
XLA Ops:
  7.2 0.0 all-gather.6.cloned.1.call-start
  7.2 0.7 all-gather.6.cloned.1.call-update
  7.9 0.0 all-gather.4.cloned.1.call-start
  8.0 0.7 convert_bitcast_fusion
  8.6 1.9 bitcast_multiply_fusion
  10.6 0.0 all-gather.4.cloned.1.call-update
  10.6 0.0 all-gather.8.cloned.1.call-start
  10.6 75.6 %all-gather.6.cloned.1.call-done = bf16[256,2048]{1,0:T(8,128)(2,1)} async-done(((bf16[8,2048]{1,0:T(8,128)(2,1)}), bf16[256,2048]{1,0:T(8,128)(2,1)}) %all-gather.6.cloned.1.call-update) | async-done | bytes 1048592 | tf_op jit(solution)/shard_map/all_gather | solution.py:114
  86.2 0.0 all-gather.8.cloned.1.call-update
  86.3 0.9 copy.11
  87.2 1.3 copy.18
  88.4 5.8 %all-to-all-start = ((bf16[32,3,64,128]{3,2,1,0:T(8,128)(2,1)}), bf16[32,3,64,128]{3,2,1,0:T(8,128)(2,1)S(1)}, u32[]{:S(2)}, u32[]{:S(2)}) async-start(bf16[32,3,64,128]{3,2,1,0:T(8,128)(2,1)} %bitcast.35), calls=%async_computation | async-start | bytes 3145728 | tf_op jit(solution)/shard_map/all_to_all | solution.py:113
  94.3 31.5 %all-gather.4.cloned.1.call-done = bf16[1024,2048]{1,0:T(8,128)(2,1)} async-done(((bf16[128,2048]{1,0:T(8,128)(2,1)}), bf16[1024,2048]{1,0:T(8,128)(2,1)}) %all-gather.4.cloned.1.call-update) | async-done | bytes 4194320 | tf_op jit(solution)/shard_map/all_gather | solution.py:116
  125.8 3.5 %convolution_convert_fusion.2 = bf16[1024,256]{1,0:T(8,128)(2,1)S(1)} fusion(bf16[1024,2048]{1,0:T(8,128)(2,1)} %all-gather.4.cloned.1.call-done, bf16[256,2048]{1,0:T(8,128)(2,1)S(1)} %copy-done.1), kind=kOutput, calls=%fused_computation.7 | convolution fusion | flops 1074003968 | bytes 5767168 | tf_op jit(solution)/shard_map/dot_general | solution.py:118
  129.3 0.0 copy-start.2
  129.3 0.3 copy.13
  129.6 21.7 %all_to_all.30 = bf16[8,256,128]{2,1,0:T(8,128)(2,1)} all-to-all(bf16[8,256,128]{2,1,0:T(8,128)(2,1)S(1)} %bitcast.41), channel_id=1, replica_groups=mesh['dp'=8,'seq'=32] {'dp'}, dimensions={0} | all-to-all | bytes 1048576 | tf_op jit(solution)/shard_map/all_to_all | solution.py:122
  151.3 4.5 %all-to-all-start.2 = ((bf16[32,64,128]{2,1,0:T(8,128)(2,1)}), bf16[32,64,128]{2,1,0:T(8,128)(2,1)S(1)}, u32[]{:S(2)}, u32[]{:S(2)}) async-start(bf16[32,64,128]{2,1,0:T(8,128)(2,1)} %bitcast.10), calls=%async_computation.2 | async-start | bytes 1048576 | tf_op jit(solution)/shard_map/all_to_all | solution.py:123
  155.8 0.1 copy.10
  155.9 14.8 %all-to-all-done.2.grad = bf16[32,64,128]{2,1,0:T(8,128)(2,1)S(1)} async-done(((bf16[32,64,128]{2,1,0:T(8,128)(2,1)}), bf16[32,64,128]{2,1,0:T(8,128)(2,1)S(1)}, u32[]{:S(2)}, u32[]{:S(2)}) %all-to-all-start.2) | async-done | bytes 524320 | tf_op jit(solution)/shard_map/all_to_all | solution.py:123
  170.8 36.8 %attention.1 = bf16[32,4,64,128]{3,2,1,0:T(8,128)(2,1)S(1)} custom-call(s32[32,8]{1,0:T(8,128)S(1)} %bitcast.36, bf16[32,3,64,128]{3,2,1,0:T(8,128)(2,1)S(1)} %all-to-all-done.qkv, bf16[32,64,128]{2,1,0:T(8,128)(2,1)S(1)} %all-to-all-done.2.grad), custom_call_target="tpu_custom_call" | custom-call | flops 3221225472 | bytes 4194304 | tf_op jit(solution)/shard_map/attention/pallas_call | solution.py:83
  207.6 53.6 %all_to_all.31 = bf16[32,4,64,128]{3,2,1,0:T(8,128)(2,1)S(1)} all-to-all(bf16[32,4,64,128]{3,2,1,0:T(8,128)(2,1)S(1)} %attention.1), channel_id=1, replica_groups=mesh['dp'=8,'seq'=32] {'seq'}, dimensions={0} | all-to-all | bytes 4194304 | tf_op jit(solution)/shard_map/all_to_all | solution.py:127
  261.2 0.2 copy.15
  261.4 15.7 %all_to_all.32 = bf16[8,256,128]{1,2,0:T(8,128)(2,1)S(1)} all-to-all(bf16[8,256,128]{1,2,0:T(8,128)(2,1)S(1)} %copy.15), channel_id=1, replica_groups=mesh['dp'=8,'seq'=32] {'dp'}, dimensions={0} | all-to-all | bytes 1048576 | tf_op jit(solution)/shard_map/all_to_all | solution.py:133
  277.1 4.4 %fusion = bf16[32,8,2048]{2,1,0:T(8,128)(2,1)} fusion(bf16[256,1024]{0,1:T(8,128)(2,1)S(1)} %bitcast.42, bf16[1024,2048]{1,0:T(8,128)(2,1)} %all-gather.4.cloned.1.call-done), kind=kOutput, calls=%fused_computation.1 | convolution fusion | flops 1074266112 | bytes 5767168 | tf_op jit(solution)/shard_map/dot_general | solution.py:137
  281.5 5.4 %all-to-all-start.5 = ((bf16[32,8,2048]{2,1,0:T(8,128)(2,1)}), bf16[32,8,2048]{2,1,0:T(8,128)(2,1)}, u32[]{:S(2)}, u32[]{:S(2)}) async-start(bf16[32,8,2048]{2,1,0:T(8,128)(2,1)} %fusion), calls=%async_computation.5 | async-start | bytes 2097152 | tf_op jit(solution)/shard_map/all_to_all | solution.py:138
  287.0 0.2 slice_bitcast_fusion
  287.2 0.1 copy.14
  287.3 1.6 copy.16
  288.9 23.9 %all-to-all-done.5 = bf16[32,8,2048]{2,1,0:T(8,128)(2,1)} async-done(((bf16[32,8,2048]{2,1,0:T(8,128)(2,1)}), bf16[32,8,2048]{2,1,0:T(8,128)(2,1)}, u32[]{:S(2)}, u32[]{:S(2)}) %all-to-all-start.5) | async-done | bytes 1048608 | tf_op jit(solution)/shard_map/all_to_all | solution.py:138
  312.8 2.0 convert_reduce_fusion
  314.8 5.5 %fusion.1 = bf16[1,128,2048]{2,1,0:T(8,128)(2,1)} fusion(bf16[2048,128]{1,0:T(8,128)(2,1)S(1)} %bitcast.38, bf16[2048,2048]{1,0:T(8,128)(2,1)} %all-gather.8.cloned.1.call-done), kind=kOutput, calls=%fused_computation.3 | convolution fusion | flops 1074003968 | bytes 9437184 | tf_op jit(solution)/shard_map/dot_general | solution.py:130
  (8 shorter events, 0.1 us)
Async XLA Ops:
  7.2 79.1 %copy-start = (bf16[1,128,6144]{2,1,0:T(8,128)(2,1)S(1)}, bf16[1,128,6144]{2,1,0:T(8,128)(2,1)}, u32[]{:S(2)}) copy-start(bf16[1,128,6144]{2,1,0:T(8,128)(2,1)} %param.5) | copy-start | bytes 4718596
  7.2 79.1 %all-gather.6.cloned.1.call-start = ((), (), s32[]{:S(2)}) async-start(), calls=%async_computation.7 | async-start | bytes 1081344 | tf_op jit(solution)/shard_map/all_gather | solution.py:114
  7.9 117.9 %all-gather.4.cloned.1.call-start = ((), (), s32[]{:S(2)}) async-start(), calls=%async_computation.6 | async-start | bytes 4718592 | tf_op jit(solution)/shard_map/all_gather | solution.py:116
  10.6 304.2 %all-gather.8.cloned.1.call-start = ((), (), s32[]{:S(2)}) async-start(), calls=%async_computation.8 | async-start | bytes 9437184 | tf_op jit(solution)/shard_map/all_gather | solution.py:117
  88.4 37.3 %copy-start.1 = (bf16[256,2048]{1,0:T(8,128)(2,1)S(1)}, bf16[256,2048]{1,0:T(8,128)(2,1)}, u32[]{:S(2)}) copy-start(bf16[256,2048]{1,0:T(8,128)(2,1)} %all-gather.6.cloned.1.call-done) | copy-start | bytes 3145732
  88.4 41.1 %all-to-all-start = ((bf16[32,3,64,128]{3,2,1,0:T(8,128)(2,1)}), bf16[32,3,64,128]{3,2,1,0:T(8,128)(2,1)S(1)}, u32[]{:S(2)}, u32[]{:S(2)}) async-start(bf16[32,3,64,128]{3,2,1,0:T(8,128)(2,1)} %bitcast.35), calls=%async_computation | async-start | bytes 3145728 | tf_op jit(solution)/shard_map/all_to_all | solution.py:113
  129.3 26.6 %copy-start.2 = (s32[1,32,8]{1,2,0:T(8,128)S(1)}, s32[1,32,8]{1,2,0:T(8,128)}, u32[]{:S(2)}) copy-start(s32[1,32,8]{1,2,0:T(8,128)} %param.9) | copy-start | bytes 3076
  151.3 19.5 %all-to-all-start.2 = ((bf16[32,64,128]{2,1,0:T(8,128)(2,1)}), bf16[32,64,128]{2,1,0:T(8,128)(2,1)S(1)}, u32[]{:S(2)}, u32[]{:S(2)}) async-start(bf16[32,64,128]{2,1,0:T(8,128)(2,1)} %bitcast.10), calls=%async_computation.2 | async-start | bytes 1048576 | tf_op jit(solution)/shard_map/all_to_all | solution.py:123
  281.5 31.3 %all-to-all-start.5 = ((bf16[32,8,2048]{2,1,0:T(8,128)(2,1)}), bf16[32,8,2048]{2,1,0:T(8,128)(2,1)}, u32[]{:S(2)}, u32[]{:S(2)}) async-start(bf16[32,8,2048]{2,1,0:T(8,128)(2,1)} %fusion), calls=%async_computation.5 | async-start | bytes 2097152 | tf_op jit(solution)/shard_map/all_to_all | solution.py:138
Sparse Core Ops, SparseCore 0:
  10.6 75.6 all-gather.5
  88.7 37.0 all-gather.3
  127.7 56.0 all-gather.7

commit v3 on v1

--- a/solution.py
+++ b/solution.py
@@ -101,46 +101,482 @@
     )(layout, qkv, grad)
 
 
+MESH = pl.DeviceIdType.MESH
+
+
+def place():
+    d, s = lax.axis_index("dp"), lax.axis_index("seq")
+    return d, d // 2, d % 2, s, s // 4, s % 4
+
+
+def shifted(z, y, k):
+    return (z + k // 4) % 8 * 4 + (y + k % 4) % 4
+
+
+def gather_kernel(
+    weight, rows, upstream, mask, qkv, grad, grads, run_weight, turned, sent,
+    w_send, w_recv, m_send, m_recv, q_send, q_recv, g_send, g_recv,
+):
+    d, x, core, s, z, y = place()
+    tokens, model = upstream.shape
+    heads, _, head, _ = qkv.shape
+    seq, runs, depth = heads, grads.shape[0], weight.shape[0]
+    own = d * (heads // runs)
+
+    def to(dp, at):
+        return {"device_id": (dp, at), "device_id_type": MESH}
+
+    barrier = pltpu.get_barrier_semaphore()
+
+    def greet_seq(k, carry):
+        pl.semaphore_signal(barrier, inc=1, **to(d, shifted(z, y, k)))
+        return carry
+
+    def greet_dp(k, carry):
+        pl.semaphore_signal(barrier, inc=1, **to((d + k) % runs, s))
+        return carry
+
+    def greet_grad(k, carry):
+        @pl.when((s // 4 != d) | (k != s))
+        def _():
+            pl.semaphore_signal(barrier, inc=1, **to(s // 4, k))
+
+        return carry
+
+    lax.fori_loop(1, seq, greet_seq, 0)
+    lax.fori_loop(1, runs, greet_dp, 0)
+    lax.fori_loop(0, seq, greet_grad, 0)
+    among = jnp.where(s // 4 == d, 1, 0)
+    pl.semaphore_wait(barrier, seq - 1 + runs - 1 + seq - among)
+
+    def weight_rows(at):
+        return run_weight.at[pl.ds(pl.multiple_of(at * depth, depth), depth)]
+
+    run_weight[pl.ds(pl.multiple_of(s * depth, depth), depth), :] = weight[...]
+
+    def weight_copy(at, k, peer):
+        return pltpu.make_async_remote_copy(
+            weight_rows(at), weight_rows(at), w_send.at[k], w_recv.at[at], **to(d, peer)
+        )
+
+    def weight_z(k, carry):
+        weight_copy(s, k, (z + k) % 8 * 4 + y).start()
+        return carry
+
+    lax.fori_loop(1, 8, weight_z, 0)
+
+    column = jnp.broadcast_to(mask[...].astype(jnp.float32), (tokens, tokens)).T.astype(jnp.bfloat16)
+    for i in range(model // tokens):
+        part = slice(i * tokens, (i + 1) * tokens)
+        grads[d, :, part] = upstream[:, part] * column
+
+    def grad_copy(run, k, peer):
+        return pltpu.make_async_remote_copy(
+            grads.at[run], grads.at[run], m_send.at[k], m_recv.at[run], **to(peer, s)
+        )
+
+    def chip(k):
+        return (x + k) % 4 * 2
+
+    def grads_x(k, carry):
+        grad_copy(d, k, chip(k) + core).start()
+        return carry
+
+    lax.fori_loop(1, 4, grads_x, 0)
+    grad_copy(d, 0, d + 1 - 2 * core).start()
+
+    def turn(pair, carry):
+        for c in range(3):
+            at = pl.multiple_of(c * (heads * head) + pair * 2 * head, 2 * head)
+            both = rows[:, pl.ds(at, 2 * head)].T
+            turned[2 * pair, c] = both[:head]
+            turned[2 * pair + 1, c] = both[head:]
+        return carry
+
+    lax.fori_loop(0, heads // 2, turn, 0)
+
+    def weight_y(k, carry):
+        at = (z + k) % 8 * 4 + y
+
+        @pl.when(k > 0)
+        def _():
+            weight_copy(at, 0, s).wait_recv()
+
+        for i in range(1, 4):
+            weight_copy(at, 8 * i + k, z * 4 + (y + i) % 4).start()
+        return carry
+
+    lax.fori_loop(0, 8, weight_y, 0)
+
+    def qkv_copy(k):
+        peer = shifted(z, y, k)
+        return pltpu.make_async_remote_copy(
+            turned.at[peer], qkv.at[s], q_send.at[k], q_recv.at[k], **to(d, peer)
+        )
+
+    def send_qkv(k, carry):
+        qkv_copy(k).start()
+        return carry
+
+    lax.fori_loop(1, seq, send_qkv, 0)
+    qkv[s] = turned[s]
+
+    def weight_wait(k, carry):
+        for i in range(1, 4):
+            weight_copy(k * 4 + (y + i) % 4, 0, s).wait_recv()
+        return carry
+
+    lax.fori_loop(0, 8, weight_wait, 0)
+
+    def context_copies(run):
+        for j in range(heads // runs):
+            yield own + j, pltpu.make_async_remote_copy(
+                sent.at[run, j], grad.at[s], g_send.at[run, j], g_recv.at[s], **to(run, own + j)
+            ), pltpu.make_async_copy(sent.at[run, j], grad.at[s], g_recv.at[s])
+
+    def one_run(run):
+        value = lax.dot_general(
+            run_weight[...], grads[run], (((1,), (1,)), ((), ())), preferred_element_type=jnp.float32
+        )
+        sent[run] = value.astype(jnp.bfloat16).reshape(heads // runs, head, tokens)
+        for peer, remote, local in context_copies(run):
+            here = (run == d) & (peer == s)
+
+            @pl.when(here)
+            def _():
+                local.start()
+
+            @pl.when(jnp.logical_not(here))
+            def _():
+                remote.start()
+
+    def runs_near(k, carry):
+        run = chip(k) + core
+
+        @pl.when(k > 0)
+        def _():
+            grad_copy(run, 0, d).wait_recv()
+            grad_copy(run, 3 + k, d + 1 - 2 * core).start()
+
+        one_run(run)
+        return carry
+
+    lax.fori_loop(0, 4, runs_near, 0)
+
+    def runs_other(k, carry):
+        run = chip(k) + 1 - core
+        grad_copy(run, 0, d).wait_recv()
+        one_run(run)
+        return carry
+
+    lax.fori_loop(0, 4, runs_other, 0)
+
+    def finish_qkv(k, carry):
+        qkv_copy(k).wait()
+        return carry
+
+    lax.fori_loop(1, seq, finish_qkv, 0)
+
+    def finish_grad(k, carry):
+        pltpu.make_async_copy(grad.at[k], grad.at[k], g_recv.at[k]).wait()
+        return carry
+
+    lax.fori_loop(0, seq, finish_grad, 0)
+
+    def finish_sent(run, carry):
+        for peer, remote, _ in context_copies(run):
+            @pl.when((run != d) | (peer != s))
+            def _():
+                remote.wait_send()
+
+        return carry
+
+    lax.fori_loop(0, runs, finish_sent, 0)
+
+    def finish_weight(k, carry):
+        weight_copy(s, k, s).wait_send()
+        return carry
+
+    lax.fori_loop(1, 32, finish_weight, 0)
+
+    def finish_grads(k, carry):
+        grad_copy(d, k, d).wait_send()
+        return carry
+
+    lax.fori_loop(0, 7, finish_grads, 0)
+
+
+def gather(weight, rows, upstream, mask, heads, runs):
+    tokens, model = upstream.shape
+    depth = weight.shape[0]
+    vmem = pl.BlockSpec(memory_space=pltpu.VMEM)
+    dma = pltpu.SemaphoreType.DMA
+    return pl.pallas_call(
+        gather_kernel,
+        name="gather",
+        out_shape=(
+            jax.ShapeDtypeStruct((heads, 3, HS, tokens), jnp.bfloat16),
+            jax.ShapeDtypeStruct((heads, HS, tokens), jnp.bfloat16),
+            jax.ShapeDtypeStruct((runs, tokens, model), jnp.bfloat16),
+            jax.ShapeDtypeStruct((heads * depth, model), jnp.bfloat16),
+        ),
+        in_specs=[vmem] * 4,
+        out_specs=(vmem,) * 4,
+        scratch_shapes=[
+            pltpu.VMEM((heads, 3, HS, tokens), jnp.bfloat16),
+            pltpu.VMEM((runs, heads // runs, HS, tokens), jnp.bfloat16),
+            dma((heads,)),
+            dma((heads,)),
+            dma((8,)),
+            dma((runs,)),
+            dma((heads,)),
+            dma((heads,)),
+            dma((runs, heads // runs)),
+            dma((heads,)),
+        ],
+        cost_estimate=pl.CostEstimate(
+            flops=2 * heads * depth * model * runs * tokens, bytes_accessed=16 << 20, transcendentals=0
+        ),
+        compiler_params=pltpu.CompilerParams(
+            collective_id=0, has_side_effects=True, vmem_limit_bytes=40 << 20
+        ),
+    )(weight, rows, upstream, mask)
+
+
+def scatter_kernel(
+    results, weight, grads, attended, rows, weight_grad,
+    context, pieces, swapped, partial, across, along,
+    c_send, c_recv, q_send, q_recv, s_send, s_recv, a_send, a_recv, l_send, l_recv,
+):
+    d, _, _, s, z, y = place()
+    heads, _, head, tokens = results.shape
+    inner, model = weight.shape
+    runs = grads.shape[0]
+    depth = weight_grad.shape[0]
+    share = inner // runs
+
+    def to(dp, at):
+        return {"device_id": (dp, at), "device_id_type": MESH}
+
+    barrier = pltpu.get_barrier_semaphore()
+
+    def greet_seq(k, carry):
+        pl.semaphore_signal(barrier, inc=1, **to(d, shifted(z, y, k)))
+        return carry
+
+    def greet_dp(k, carry):
+        pl.semaphore_signal(barrier, inc=1, **to((d + k) % runs, s))
+        return carry
+
+    lax.fori_loop(1, heads, greet_seq, 0)
+    lax.fori_loop(1, runs, greet_dp, 0)
+    pl.semaphore_wait(barrier, heads - 1 + runs - 1)
+
+    def context_copy(k):
+        peer = shifted(z, y, k)
+        return pltpu.make_async_remote_copy(
+            results.at[peer, 0], context.at[s], c_send.at[k], c_recv.at[k], **to(d, peer)
+        )
+
+    def piece_copy(k):
+        peer = shifted(z, y, k)
+        return pltpu.make_async_remote_copy(
+            results.at[peer, pl.ds(1, 3)], pieces.at[s], q_send.at[k], q_recv.at[k], **to(d, peer)
+        )
+
+    def send_context(k, carry):
+        context_copy(k).start()
+        return carry
+
+    def send_pieces(k, carry):
+        piece_copy(k).start()
+        return carry
+
+    lax.fori_loop(1, heads, send_context, 0)
+    lax.fori_loop(1, heads, send_pieces, 0)
+    context[s] = results[s, 0]
+    pieces[s] = results[s, 1:4]
+
+    def wait_context(k, carry):
+        context_copy(k).wait_recv()
+        return carry
+
+    lax.fori_loop(1, heads, wait_context, 0)
+
+    group = heads // runs
+
+    def swap_copy(k):
+        peer = (d + k) % runs
+        return pltpu.make_async_remote_copy(
+            context.at[pl.ds(peer * group, group)], swapped.at[d], s_send.at[k], s_recv.at[k], **to(peer, s)
+        )
+
+    def send_swap(k, carry):
+        swap_copy(k).start()
+        return carry
+
+    lax.fori_loop(1, runs, send_swap, 0)
+    swapped[d] = context[pl.ds(d * group, group)]
+
+    wide = 512
+
+    def attend(i, carry):
+        at = pl.ds(pl.multiple_of(i * wide, wide), wide)
+        attended[:, at] = lax.dot_general(
+            context[...].reshape(inner, tokens),
+            weight[:, at],
+            (((0,), (0,)), ((), ())),
+            preferred_element_type=jnp.float32,
+        ).astype(jnp.bfloat16)
+        return carry
+
+    lax.fori_loop(0, model // wide, attend, 0)
+
+    def wait_swap(k, carry):
+        swap_copy(k).wait_recv()
+        return carry
+
+    lax.fori_loop(1, runs, wait_swap, 0)
+
+    def multiply(i, carry):
+        at = pl.ds(pl.multiple_of(i * wide, wide), wide)
+        total = jnp.zeros((share, wide), jnp.float32)
+        for r in range(runs):
+            total += jnp.dot(
+                swapped[r].reshape(share, tokens), grads[r, :, at], preferred_element_type=jnp.float32
+            )
+        total = total.astype(jnp.bfloat16)
+        for k in range(heads):
+            partial[k % 4, k // 4, :, at] = total[k * depth : (k + 1) * depth]
+        return carry
+
+    lax.fori_loop(0, model // wide, multiply, 0)
+
+    def across_copy(k):
+        peer = (y + k) % 4
+        return pltpu.make_async_remote_copy(
+            partial.at[peer], across.at[k], a_send.at[k], a_recv.at[k], **to(d, z * 4 + peer)
+        )
+
+    for k in range(1, 4):
+        across_copy(k).start()
+    for k in range(1, 4):
+        across_copy(k).wait_recv()
+
+    def add_across(k, carry):
+        total = partial[y, k].astype(jnp.float32)
+        for i in range(1, 4):
+            total += across[i, k].astype(jnp.float32)
+        across[0, k] = total.astype(jnp.bfloat16)
+        return carry
+
+    def along_copy(k):
+        peer = (z + k) % 8
+        return pltpu.make_async_remote_copy(
+            across.at[0, peer], along.at[k], l_send.at[k], l_recv.at[k], **to(d, peer * 4 + y)
+        )
+
+    def send_along(k, carry):
+        along_copy(k).start()
+        return carry
+
+    lax.fori_loop(0, 8, add_across, 0)
+    lax.fori_loop(1, 8, send_along, 0)
+
+    def wait_pieces(k, carry):
+        piece_copy(k).wait_recv()
+        return carry
+
+    lax.fori_loop(1, heads, wait_pieces, 0)
+
+    def turn(pair, carry):
+        for c in range(3):
+            at = pl.multiple_of(c * inner + pair * 2 * head, 2 * head)
+            both = jnp.concatenate([pieces[2 * pair, c], pieces[2 * pair + 1, c]], 0)
+            rows[:, pl.ds(at, 2 * head)] = both.T
+        return carry
+
+    lax.fori_loop(0, heads // 2, turn, 0)
+
+    def wait_along(k, carry):
+        along_copy(k).wait_recv()
+        return carry
+
+    lax.fori_loop(1, 8, wait_along, 0)
+    total = across[0, z].astype(jnp.float32)
+    for k in range(1, 8):
+        total += along[k].astype(jnp.float32)
+    weight_grad[...] = total
+
+    def finish_seq(k, carry):
+        context_copy(k).wait_send()
+        piece_copy(k).wait_send()
+        return carry
+
+    def finish_swap(k, carry):
+        swap_copy(k).wait_send()
+        return carry
+
+    def finish_along(k, carry):
+        along_copy(k).wait_send()
+        return carry
+
+    lax.fori_loop(1, heads, finish_seq, 0)
+    lax.fori_loop(1, runs, finish_swap, 0)
+    for k in range(1, 4):
+        across_copy(k).wait_send()
+    lax.fori_loop(1, 8, finish_along, 0)
+
+
+def scatter(results, weight, grads, depth):
+    heads, _, head, tokens = results.shape
+    inner, model = weight.shape
+    runs = grads.shape[0]
+    bf16, dma = jnp.bfloat16, pltpu.SemaphoreType.DMA
+    vmem = pl.BlockSpec(memory_space=pltpu.VMEM)
+    return pl.pallas_call(
+        scatter_kernel,
+        name="scatter",
+        out_shape=(
+            jax.ShapeDtypeStruct((tokens, model), bf16),
+            jax.ShapeDtypeStruct((tokens, 3 * inner), bf16),
+            jax.ShapeDtypeStruct((depth, model), jnp.float32),
+        ),
+        in_specs=[vmem] * 3,
+        out_specs=(vmem,) * 3,
+        scratch_shapes=[
+            pltpu.VMEM((heads, head, tokens), bf16),
+            pltpu.VMEM((heads, 3, head, tokens), bf16),
+            pltpu.VMEM((runs, heads // runs, head, tokens), bf16),
+            pltpu.VMEM((4, 8, depth, model), bf16),
+            pltpu.VMEM((4, 8, depth, model), bf16),
+            pltpu.VMEM((8, depth, model), bf16),
+            dma((heads,)), dma((heads,)), dma((heads,)), dma((heads,)),
+            dma((runs,)), dma((runs,)), dma((4,)), dma((4,)), dma((8,)), dma((8,)),
+        ],
+        cost_estimate=pl.CostEstimate(
+            flops=4 * inner * model * tokens, bytes_accessed=20 << 20, transcendentals=0
+        ),
+        compiler_params=pltpu.CompilerParams(
+            collective_id=1, has_side_effects=True, vmem_limit_bytes=56 << 20
+        ),
+    )(results, weight, grads)
+
+
 def on_device(projected, out_weight, upstream, peak_mask, block_layout):
-    tokens = projected.shape[1]
     inner = projected.shape[2] // 3
     heads = inner // HS
-    model = out_weight.shape[1]
     dp = lax.axis_size("dp")
-    seq = lax.axis_size("seq")
-
-    turned = projected[0].T.reshape(3, heads, HS, tokens).transpose(1, 0, 2, 3)
-    qkv = lax.all_to_all(turned, "seq", split_axis=0, concat_axis=0, tiled=True)
-    full_weight = lax.all_gather(out_weight, ("dp", "seq"), axis=0, tiled=True)
-    masked_grad = upstream[0] * peak_mask[0][:, None].astype(jnp.bfloat16)
-    run_grads = lax.all_gather(masked_grad, "dp", axis=0, tiled=True)
-    grad_context = lax.dot_general(
-        full_weight, masked_grad, (((1,), (1,)), ((), ())), preferred_element_type=jnp.float32
-    ).astype(jnp.bfloat16)
-    grad_heads = lax.all_to_all(
-        grad_context.reshape(heads, HS, tokens), "seq", split_axis=0, concat_axis=0, tiled=True
+
+    qkv, grad_heads, run_grads, run_weight = gather(
+        out_weight, projected[0], upstream[0], peak_mask, heads, dp
     )
+    full_weight = lax.all_gather(run_weight, "dp", axis=0, tiled=True)
     results = attention(block_layout[0], qkv, grad_heads)
-    back = lax.all_to_all(results, "seq", split_axis=0, concat_axis=0, tiled=True)
-    context = back[:, 0].reshape(inner, tokens)
-    projected_grad = back[:, 1:].transpose(3, 1, 0, 2).reshape(1, tokens, 3 * inner)
-    attended = lax.dot_general(
-        context, full_weight, (((0,), (0,)), ((), ())), preferred_element_type=jnp.float32
-    ).astype(jnp.bfloat16)
-    run_context = lax.all_to_all(
-        context.reshape(dp, inner // dp, tokens), "dp", split_axis=0, concat_axis=0, tiled=True
+    attended, projected_grad, weight_grad = scatter(
+        results, full_weight, run_grads, out_weight.shape[0]
     )
-    run_context = run_context.transpose(1, 0, 2).reshape(inner // dp, dp * tokens)
-    partial = jnp.dot(run_context, run_grads, preferred_element_type=jnp.float32)
-    pieces = lax.all_to_all(
-        partial.astype(jnp.bfloat16).reshape(seq, inner // (dp * seq), model),
-        "seq",
-        split_axis=0,
-        concat_axis=0,
-        tiled=True,
-    )
-    weight_grad = jnp.sum(pieces.astype(jnp.float32), axis=0)
-    return (attended.reshape(1, tokens, model), projected_grad, weight_grad)
+    return (attended[None], projected_grad[None], weight_grad)
 
 
 def solution(mesh):

time: 322 us -> 243 us (0.75)
  Pallas kernels: 36.8 us -> 199 us
  waiting for transfers between devices: 158 us -> 17.5 us
  blocking collectives: 52.9 us -> 0 us
  starting transfers between devices: 30.6 us -> 0.04 us
  matrix products: 16.4 us -> 0 us
  local copies, waits for them, and re-layouts: 7.19 us -> 12.4 us
    pallas_call x0 -> x2, Pallas kernels: none -> 162 us  [the longest x1 88 us: gather(): pl.pallas_call(gather_kernel, name='gather', out_shape=(jax.ShapeDtypeStr...]
    all_gather x2 -> x1, waiting for transfers between devices: 113 us -> 17.5 us  [on_device(): full_weight = lax.all_gather(run_weight, 'dp', axis=0, tiled=True)]
    all_to_all x1 -> x0, blocking collectives: 52.9 us -> none  [on_device(): lax.all_to_all(results, 'seq', split_axis=0, concat_axis=0, tiled=True)]
    all_to_all x4 -> x0, waiting for transfers between devices: 44.7 us -> none  [the longest x1 18.7 us: on_device(): lax.all_to_all(partial.astype(jnp.bfloat16).reshape(seq, inner // (dp * s...]
    all_to_all x4 -> x0, starting transfers between devices: 30.6 us -> none  [the longest x1 12.2 us: on_device(): qkv = lax.all_to_all(turned, 'seq', split_axis=0, concat_axis=0, tiled=True)]
    dot_general x3 -> x0, matrix products: 16.4 us -> none  [the longest x1 6.44 us: on_device(): lax.dot_general(full_weight, masked_grad, (((1,), (1,)), ((), ())), prefe...]
    unnamed x9 -> x20, local copies, waits for them, and re-layouts: 3.57 us -> 12.4 us
  transfers between devices with their start and end apart: 6 -> 1, of which waited for: 4 -> 1; matrix products, arithmetic and copies ran while one was open for 6% -> 0% of each run, Pallas kernels for 12% -> 15%
where the time goes in v3:
time: 243 us
  Pallas kernels  199 us (82%)
  waiting for transfers between devices  17.5 us (7%)
  between operations  14.1 us (6%)
  local copies, waits for them, and re-layouts  12.4 us (5%)
    pallas_call x1, Pallas kernels, gather(): pl.pallas_call(gather_kernel, name='gather', out_shape=(jax.ShapeDtypeStr...  88 us
    pallas_call x1, Pallas kernels, scatter(): pl.pallas_call(scatter_kernel, name='scatter', out_shape=(jax.ShapeDtypeS...  74 us
    pallas_call x1, Pallas kernels, attention(): pl.pallas_call(attention_kernel, name='attention', out_shape=jax.ShapeDty...  36.8 us
    all_gather x1, waiting for transfers between devices, on_device(): full_weight = lax.all_gather(run_weight, 'dp', axis=0, tiled=True)  17.5 us
    unnamed x20, local copies, waits for them, and re-layouts  12.4 us
  transfers between devices with their start and end apart: 1, of which 1 were waited for; matrix products, arithmetic and copies ran while one was open for 0% of the time, Pallas kernels for 15%

profile of v3, /device:TPU:1, one launch (start us, length us, event | category | flops | bytes accessed | tf_op | source)
XLA Modules:
  0.0 242.9 jit_solution(8457441814527586472)
XLA Ops:
  7.2 0.0 all-gather.2.cloned.1.call-start
  7.2 0.0 copy-start.2
  7.2 1.4 copy-done.2
  8.6 0.0 copy-start.3
  8.6 1.0 copy-done.3
  9.7 0.0 copy-start.4
  9.7 0.8 copy-done.4
  10.4 0.0 copy-start.5
  10.4 0.7 copy-done.5
  11.1 0.0 copy-start.7
  11.1 88.0 %gather.1 = (bf16[32,3,64,128]{3,2,1,0:T(8,128)(2,1)S(1)}, bf16[32,64,128]{2,1,0:T(8,128)(2,1)S(1)}, bf16[8,128,2048]{2,1,0:T(8,128)(2,1)S(1)}, bf16[256,2048]{1,0:T(8,128)(2,1)}) custom-call(bf16[8,2048]{1,0:T(8,128)(2,1)S(1)} %copy-done.4, bf16[128,6144]{1,0:T(8,128)(2,1)S(1)} %bitcast.6, bf16[128,2048]{1,0:T(8,128)(2,1)S(1)} %bitcast.7, ...), custom_call_target="tpu_custom_call" | custom-call | flops 1073741824 | bytes 16777216 | tf_op jit(solution)/shard_map/gather/pallas_call | solution.py:314
  99.1 0.0 copy-start
  99.1 1.9 copy-done
  101.1 0.0 all-gather.2.cloned.1.call-update
  101.1 0.0 copy-done.7
  101.1 0.1 copy.8
  101.2 36.8 %attention.1.results = bf16[32,4,64,128]{3,2,1,0:T(8,128)(2,1)S(1)} custom-call(s32[32,8]{1,0:T(8,128)S(1)} %bitcast.5, bf16[32,3,64,128]{3,2,1,0:T(8,128)(2,1)S(1)} %get-tuple-element.10.qkv, bf16[32,64,128]{2,1,0:T(8,128)(2,1)S(1)} %get-tuple-element.11.grad), custom_call_target="tpu_custom_call" | custom-call | flops 3221225472 | bytes 4194304 | tf_op jit(solution)/shard_map/attention/pallas_call | solution.py:83
  138.0 0.0 copy-start.1
  138.0 1.3 copy-done.1
  139.3 17.5 %all-gather.2.cloned.1.call-done.weight = bf16[2048,2048]{1,0:T(8,128)(2,1)} async-done(((bf16[256,2048]{1,0:T(8,128)(2,1)}), bf16[2048,2048]{1,0:T(8,128)(2,1)}) %all-gather.2.cloned.1.call-update) | async-done | bytes 8388624 | tf_op jit(solution)/shard_map/all_gather | solution.py:574
  156.8 74.0 %scatter.1 = (bf16[128,2048]{1,0:T(8,128)(2,1)}, bf16[128,6144]{1,0:T(8,128)(2,1)}, f32[8,2048]{1,0:T(8,128)}) custom-call(bf16[32,4,64,128]{3,2,1,0:T(8,128)(2,1)} %copy-done.1, bf16[2048,2048]{1,0:T(8,128)(2,1)} %all-gather.2.cloned.1.call-done.weight, bf16[8,128,2048]{2,1,0:T(8,128)(2,1)} %copy-done), custom_call_target="tpu_custom_call" | custom-call | flops 2147483648 | bytes 20971520 | tf_op jit(solution)/shard_map/scatter/pallas_call | solution.py:537
  230.8 1.9 copy.12
  232.7 0.0 copy-start.6
  232.7 2.7 %copy.13 = bf16[1,128,6144]{2,1,0:T(8,128)(2,1)} copy(bf16[1,128,6144]{2,1,0:T(8,128)(2,1)} %bitcast.8) | data formatting | bytes 3145728
  235.4 0.0 copy-done.6
  235.4 0.6 copy.14
Async XLA Ops:
  7.2 149.6 %all-gather.2.cloned.1.call-start = ((), (), s32[]{:S(2)}) async-start(), calls=%async_computation | async-start | bytes 9437184 | tf_op jit(solution)/shard_map/all_gather | solution.py:574
  7.2 1.4 copy-start.2
  8.6 1.0 copy-start.3
  9.7 0.8 copy-start.4
  10.4 0.7 copy-start.5
  11.1 90.0 %copy-start.7 = (s32[1,32,8]{1,2,0:T(8,128)S(1)}, s32[1,32,8]{1,2,0:T(8,128)}, u32[]{:S(2)}) copy-start(s32[1,32,8]{1,2,0:T(8,128)} %param.9) | copy-start | bytes 3076
  99.1 2.0 copy-start
  138.0 1.3 copy-start.1
  232.7 2.7 %copy-start.6 = (f32[8,2048]{1,0:T(8,128)S(1)}, f32[8,2048]{1,0:T(8,128)}, u32[]{:S(2)}) copy-start(f32[8,2048]{1,0:T(8,128)} %get-tuple-element.22) | copy-start | bytes 196612
Sparse Core Ops, SparseCore 0:
  101.2 55.5 all-gather.1

commit v4 on v3

--- a/solution.py
+++ b/solution.py
@@ -110,22 +110,36 @@
 
 
 def shifted(z, y, k):
-    return (z + k // 4) % 8 * 4 + (y + k % 4) % 4
+    along, across = k // 4, k % 4
+    along = 4 + (1 - along % 2 * 2) * ((along + 1) // 2)
+    across = 2 + (1 - across % 2 * 2) * ((across + 1) // 2)
+    return (z + along) % 8 * 4 + (y + across) % 4
 
 
 def gather_kernel(
-    weight, rows, upstream, mask, qkv, grad, grads, run_weight, turned, sent,
-    w_send, w_recv, m_send, m_recv, q_send, q_recv, g_send, g_recv,
+    weight, rows_in, upstream_in, mask_in, qkv, grad, grads, run_weight,
+    rows, upstream, mask, turned, sent, mixed,
+    in_sem, w_send, w_recv, m_send, m_recv, q_send, q_recv, x_send, x_recv, g_send, g_recv,
 ):
     d, x, core, s, z, y = place()
     tokens, model = upstream.shape
     heads, _, head, _ = qkv.shape
     seq, runs, depth = heads, grads.shape[0], weight.shape[0]
-    own = d * (heads // runs)
 
     def to(dp, at):
         return {"device_id": (dp, at), "device_id_type": MESH}
 
+    def weight_rows(at):
+        return run_weight.at[pl.ds(pl.multiple_of(at * depth, depth), depth)]
+
+    loads = [
+        pltpu.make_async_copy(upstream_in, upstream, in_sem.at[0]),
+        pltpu.make_async_copy(mask_in, mask, in_sem.at[1]),
+        pltpu.make_async_copy(rows_in, rows, in_sem.at[2]),
+        pltpu.make_async_copy(weight, weight_rows(s), in_sem.at[3]),
+    ]
+    for load in loads:
+        load.start()
     barrier = pltpu.get_barrier_semaphore()
 
     def greet_seq(k, carry):
@@ -136,54 +150,14 @@
         pl.semaphore_signal(barrier, inc=1, **to((d + k) % runs, s))
         return carry
 
-    def greet_grad(k, carry):
-        @pl.when((s // 4 != d) | (k != s))
-        def _():
-            pl.semaphore_signal(barrier, inc=1, **to(s // 4, k))
-
-        return carry
-
-    lax.fori_loop(1, seq, greet_seq, 0)
+    lax.fori_loop(0, seq - 1, greet_seq, 0)
     lax.fori_loop(1, runs, greet_dp, 0)
-    lax.fori_loop(0, seq, greet_grad, 0)
-    among = jnp.where(s // 4 == d, 1, 0)
-    pl.semaphore_wait(barrier, seq - 1 + runs - 1 + seq - among)
-
-    def weight_rows(at):
-        return run_weight.at[pl.ds(pl.multiple_of(at * depth, depth), depth)]
-
-    run_weight[pl.ds(pl.multiple_of(s * depth, depth), depth), :] = weight[...]
-
-    def weight_copy(at, k, peer):
-        return pltpu.make_async_remote_copy(
-            weight_rows(at), weight_rows(at), w_send.at[k], w_recv.at[at], **to(d, peer)
-        )
-
-    def weight_z(k, carry):
-        weight_copy(s, k, (z + k) % 8 * 4 + y).start()
-        return carry
-
-    lax.fori_loop(1, 8, weight_z, 0)
-
+    loads[0].wait()
+    loads[1].wait()
     column = jnp.broadcast_to(mask[...].astype(jnp.float32), (tokens, tokens)).T.astype(jnp.bfloat16)
     for i in range(model // tokens):
         part = slice(i * tokens, (i + 1) * tokens)
         grads[d, :, part] = upstream[:, part] * column
-
-    def grad_copy(run, k, peer):
-        return pltpu.make_async_remote_copy(
-            grads.at[run], grads.at[run], m_send.at[k], m_recv.at[run], **to(peer, s)
-        )
-
-    def chip(k):
-        return (x + k) % 4 * 2
-
-    def grads_x(k, carry):
-        grad_copy(d, k, chip(k) + core).start()
-        return carry
-
-    lax.fori_loop(1, 4, grads_x, 0)
-    grad_copy(d, 0, d + 1 - 2 * core).start()
 
     def turn(pair, carry):
         for c in range(3):
@@ -193,7 +167,50 @@
             turned[2 * pair + 1, c] = both[head:]
         return carry
 
+    loads[2].wait()
     lax.fori_loop(0, heads // 2, turn, 0)
+    loads[3].wait()
+
+    pl.semaphore_wait(barrier, seq - 1 + runs - 1)
+
+    def weight_copy(at, k, peer):
+        return pltpu.make_async_remote_copy(
+            weight_rows(at), weight_rows(at), w_send.at[k], w_recv.at[at], **to(d, peer)
+        )
+
+    def weight_z(k, carry):
+        weight_copy(s, k, (z + k) % 8 * 4 + y).start()
+        return carry
+
+    lax.fori_loop(1, 8, weight_z, 0)
+
+    def grad_copy(run, k, peer):
+        return pltpu.make_async_remote_copy(
+            grads.at[run], grads.at[run], m_send.at[k], m_recv.at[run], **to(peer, s)
+        )
+
+    def chip(k):
+        return (x + k) % 4 * 2
+
+    def grads_x(k, carry):
+        grad_copy(d, k, chip(k) + core).start()
+        return carry
+
+    lax.fori_loop(1, 4, grads_x, 0)
+    grad_copy(d, 0, d + 1 - 2 * core).start()
+
+    def qkv_copy(k):
+        peer = shifted(z, y, k)
+        return pltpu.make_async_remote_copy(
+            turned.at[peer], qkv.at[s], q_send.at[k], q_recv.at[k], **to(d, peer)
+        )
+
+    def send_qkv(k, carry):
+        qkv_copy(k).start()
+        return carry
+
+    lax.fori_loop(0, seq - 1, send_qkv, 0)
+    qkv[s] = turned[s]
 
     def weight_y(k, carry):
         at = (z + k) % 8 * 4 + y
@@ -208,19 +225,6 @@
 
     lax.fori_loop(0, 8, weight_y, 0)
 
-    def qkv_copy(k):
-        peer = shifted(z, y, k)
-        return pltpu.make_async_remote_copy(
-            turned.at[peer], qkv.at[s], q_send.at[k], q_recv.at[k], **to(d, peer)
-        )
-
-    def send_qkv(k, carry):
-        qkv_copy(k).start()
-        return carry
-
-    lax.fori_loop(1, seq, send_qkv, 0)
-    qkv[s] = turned[s]
-
     def weight_wait(k, carry):
         for i in range(1, 4):
             weight_copy(k * 4 + (y + i) % 4, 0, s).wait_recv()
@@ -228,27 +232,20 @@
 
     lax.fori_loop(0, 8, weight_wait, 0)
 
-    def context_copies(run):
-        for j in range(heads // runs):
-            yield own + j, pltpu.make_async_remote_copy(
-                sent.at[run, j], grad.at[s], g_send.at[run, j], g_recv.at[s], **to(run, own + j)
-            ), pltpu.make_async_copy(sent.at[run, j], grad.at[s], g_recv.at[s])
+    def sent_copy(run, source):
+        return pltpu.make_async_remote_copy(
+            sent.at[run], mixed.at[source], x_send.at[run], x_recv.at[source], **to(run, s)
+        )
 
     def one_run(run):
         value = lax.dot_general(
             run_weight[...], grads[run], (((1,), (1,)), ((), ())), preferred_element_type=jnp.float32
         )
         sent[run] = value.astype(jnp.bfloat16).reshape(heads // runs, head, tokens)
-        for peer, remote, local in context_copies(run):
-            here = (run == d) & (peer == s)
-
-            @pl.when(here)
-            def _():
-                local.start()
-
-            @pl.when(jnp.logical_not(here))
-            def _():
-                remote.start()
+
+        @pl.when(run != d)
+        def _():
+            sent_copy(run, d).start()
 
     def runs_near(k, carry):
         run = chip(k) + core
@@ -271,27 +268,40 @@
 
     lax.fori_loop(0, 4, runs_other, 0)
 
-    def finish_qkv(k, carry):
+    mixed[d] = sent[d]
+
+    def wait_mixed(k, carry):
+        sent_copy(d, (d + k) % runs).wait_recv()
+        return carry
+
+    lax.fori_loop(1, runs, wait_mixed, 0)
+
+    def head_copy(k):
+        peer = shifted(z, y, k)
+        share = heads // runs
+        return pltpu.make_async_remote_copy(
+            mixed.at[peer // share, peer % share], grad.at[s], g_send.at[k], g_recv.at[k], **to(d, peer)
+        )
+
+    def send_head(k, carry):
+        head_copy(k).start()
+        return carry
+
+    lax.fori_loop(0, seq - 1, send_head, 0)
+    grad[s] = mixed[s // (heads // runs), s % (heads // runs)]
+
+    def finish_seq(k, carry):
         qkv_copy(k).wait()
-        return carry
-
-    lax.fori_loop(1, seq, finish_qkv, 0)
-
-    def finish_grad(k, carry):
-        pltpu.make_async_copy(grad.at[k], grad.at[k], g_recv.at[k]).wait()
-        return carry
-
-    lax.fori_loop(0, seq, finish_grad, 0)
-
-    def finish_sent(run, carry):
-        for peer, remote, _ in context_copies(run):
-            @pl.when((run != d) | (peer != s))
-            def _():
-                remote.wait_send()
-
-        return carry
-
-    lax.fori_loop(0, runs, finish_sent, 0)
+        head_copy(k).wait()
+        return carry
+
+    lax.fori_loop(0, seq - 1, finish_seq, 0)
+
+    def finish_sent(k, carry):
+        sent_copy((d + k) % runs, d).wait_send()
+        return carry
+
+    lax.fori_loop(1, runs, finish_sent, 0)
 
     def finish_weight(k, carry):
         weight_copy(s, k, s).wait_send()
@@ -320,40 +330,47 @@
             jax.ShapeDtypeStruct((runs, tokens, model), jnp.bfloat16),
             jax.ShapeDtypeStruct((heads * depth, model), jnp.bfloat16),
         ),
-        in_specs=[vmem] * 4,
+        in_specs=[pl.BlockSpec(memory_space=pltpu.HBM)] * 4,
         out_specs=(vmem,) * 4,
         scratch_shapes=[
+            pltpu.VMEM(rows.shape, jnp.bfloat16),
+            pltpu.VMEM(upstream.shape, jnp.bfloat16),
+            pltpu.VMEM(mask.shape, jnp.int32),
             pltpu.VMEM((heads, 3, HS, tokens), jnp.bfloat16),
             pltpu.VMEM((runs, heads // runs, HS, tokens), jnp.bfloat16),
+            pltpu.VMEM((runs, heads // runs, HS, tokens), jnp.bfloat16),
+            dma((4,)),
             dma((heads,)),
             dma((heads,)),
             dma((8,)),
             dma((runs,)),
             dma((heads,)),
             dma((heads,)),
-            dma((runs, heads // runs)),
+            dma((runs,)),
+            dma((runs,)),
+            dma((heads,)),
             dma((heads,)),
         ],
         cost_estimate=pl.CostEstimate(
             flops=2 * heads * depth * model * runs * tokens, bytes_accessed=16 << 20, transcendentals=0
         ),
         compiler_params=pltpu.CompilerParams(
-            collective_id=0, has_side_effects=True, vmem_limit_bytes=40 << 20
+            collective_id=0, has_side_effects=True, vmem_limit_bytes=24 << 20
         ),
     )(weight, rows, upstream, mask)
 
 
 def scatter_kernel(
-    results, weight, grads, attended, rows, weight_grad,
-    context, pieces, swapped, partial, across, along,
+    results, grads, context, pieces, weight_grad,
+    swapped, partial, across, along,
     c_send, c_recv, q_send, q_recv, s_send, s_recv, a_send, a_recv, l_send, l_recv,
 ):
     d, _, _, s, z, y = place()
     heads, _, head, tokens = results.shape
-    inner, model = weight.shape
-    runs = grads.shape[0]
+    runs, _, model = grads.shape
+    group = heads // runs
+    share = group * head
     depth = weight_grad.shape[0]
-    share = inner // runs
 
     def to(dp, at):
         return {"device_id": (dp, at), "device_id_type": MESH}
@@ -368,7 +385,7 @@
         pl.semaphore_signal(barrier, inc=1, **to((d + k) % runs, s))
         return carry
 
-    lax.fori_loop(1, heads, greet_seq, 0)
+    lax.fori_loop(0, heads - 1, greet_seq, 0)
     lax.fori_loop(1, runs, greet_dp, 0)
     pl.semaphore_wait(barrier, heads - 1 + runs - 1)
 
@@ -381,7 +398,7 @@
     def piece_copy(k):
         peer = shifted(z, y, k)
         return pltpu.make_async_remote_copy(
-            results.at[peer, pl.ds(1, 3)], pieces.at[s], q_send.at[k], q_recv.at[k], **to(d, peer)
+            results.at[peer, pl.ds(1, 3)], pieces.at[:, s], q_send.at[k], q_recv.at[k], **to(d, peer)
         )
 
     def send_context(k, carry):
@@ -392,18 +409,16 @@
         piece_copy(k).start()
         return carry
 
-    lax.fori_loop(1, heads, send_context, 0)
-    lax.fori_loop(1, heads, send_pieces, 0)
+    lax.fori_loop(0, heads - 1, send_context, 0)
     context[s] = results[s, 0]
-    pieces[s] = results[s, 1:4]
+    pieces[:, s] = results[s, 1:4]
 
     def wait_context(k, carry):
         context_copy(k).wait_recv()
         return carry
 
-    lax.fori_loop(1, heads, wait_context, 0)
-
-    group = heads // runs
+    lax.fori_loop(0, heads - 1, wait_context, 0)
+    lax.fori_loop(0, heads - 1, send_pieces, 0)
 
     def swap_copy(k):
         peer = (d + k) % runs
@@ -418,34 +433,19 @@
     lax.fori_loop(1, runs, send_swap, 0)
     swapped[d] = context[pl.ds(d * group, group)]
 
-    wide = 512
-
-    def attend(i, carry):
-        at = pl.ds(pl.multiple_of(i * wide, wide), wide)
-        attended[:, at] = lax.dot_general(
-            context[...].reshape(inner, tokens),
-            weight[:, at],
-            (((0,), (0,)), ((), ())),
-            preferred_element_type=jnp.float32,
-        ).astype(jnp.bfloat16)
-        return carry
-
-    lax.fori_loop(0, model // wide, attend, 0)
-
     def wait_swap(k, carry):
         swap_copy(k).wait_recv()
         return carry
 
     lax.fori_loop(1, runs, wait_swap, 0)
 
+    wide = 512
+
     def multiply(i, carry):
         at = pl.ds(pl.multiple_of(i * wide, wide), wide)
-        total = jnp.zeros((share, wide), jnp.float32)
-        for r in range(runs):
-            total += jnp.dot(
-                swapped[r].reshape(share, tokens), grads[r, :, at], preferred_element_type=jnp.float32
-            )
-        total = total.astype(jnp.bfloat16)
+        left = jnp.concatenate([swapped[r].reshape(share, tokens) for r in range(runs)], 1)
+        right = grads[:, :, at].reshape(runs * tokens, wide)
+        total = jnp.dot(left, right, preferred_element_type=jnp.float32).astype(jnp.bfloat16)
         for k in range(heads):
             partial[k % 4, k // 4, :, at] = total[k * depth : (k + 1) * depth]
         return carry
@@ -460,6 +460,7 @@
 
     for k in range(1, 4):
         across_copy(k).start()
+
     for k in range(1, 4):
         across_copy(k).wait_recv()
 
@@ -487,17 +488,6 @@
         piece_copy(k).wait_recv()
         return carry
 
-    lax.fori_loop(1, heads, wait_pieces, 0)
-
-    def turn(pair, carry):
-        for c in range(3):
-            at = pl.multiple_of(c * inner + pair * 2 * head, 2 * head)
-            both = jnp.concatenate([pieces[2 * pair, c], pieces[2 * pair + 1, c]], 0)
-            rows[:, pl.ds(at, 2 * head)] = both.T
-        return carry
-
-    lax.fori_loop(0, heads // 2, turn, 0)
-
     def wait_along(k, carry):
         along_copy(k).wait_recv()
         return carry
@@ -507,6 +497,7 @@
     for k in range(1, 8):
         total += along[k].astype(jnp.float32)
     weight_grad[...] = total
+    lax.fori_loop(0, heads - 1, wait_pieces, 0)
 
     def finish_seq(k, carry):
         context_copy(k).wait_send()
@@ -521,32 +512,29 @@
         along_copy(k).wait_send()
         return carry
 
-    lax.fori_loop(1, heads, finish_seq, 0)
+    lax.fori_loop(0, heads - 1, finish_seq, 0)
     lax.fori_loop(1, runs, finish_swap, 0)
     for k in range(1, 4):
         across_copy(k).wait_send()
     lax.fori_loop(1, 8, finish_along, 0)
 
 
-def scatter(results, weight, grads, depth):
+def scatter(results, grads, depth):
     heads, _, head, tokens = results.shape
-    inner, model = weight.shape
-    runs = grads.shape[0]
+    runs, _, model = grads.shape
     bf16, dma = jnp.bfloat16, pltpu.SemaphoreType.DMA
     vmem = pl.BlockSpec(memory_space=pltpu.VMEM)
     return pl.pallas_call(
         scatter_kernel,
         name="scatter",
         out_shape=(
-            jax.ShapeDtypeStruct((tokens, model), bf16),
-            jax.ShapeDtypeStruct((tokens, 3 * inner), bf16),
+            jax.ShapeDtypeStruct((heads, head, tokens), bf16),
+            jax.ShapeDtypeStruct((3, heads, head, tokens), bf16),
             jax.ShapeDtypeStruct((depth, model), jnp.float32),
         ),
-        in_specs=[vmem] * 3,
+        in_specs=[vmem] * 2,
         out_specs=(vmem,) * 3,
         scratch_shapes=[
-            pltpu.VMEM((heads, head, tokens), bf16),
-            pltpu.VMEM((heads, 3, head, tokens), bf16),
             pltpu.VMEM((runs, heads // runs, head, tokens), bf16),
             pltpu.VMEM((4, 8, depth, model), bf16),
             pltpu.VMEM((4, 8, depth, model), bf16),
@@ -555,12 +543,12 @@
             dma((runs,)), dma((runs,)), dma((4,)), dma((4,)), dma((8,)), dma((8,)),
         ],
         cost_estimate=pl.CostEstimate(
-            flops=4 * inner * model * tokens, bytes_accessed=20 << 20, transcendentals=0
+            flops=2 * heads * head * model * tokens, bytes_accessed=20 << 20, transcendentals=0
         ),
         compiler_params=pltpu.CompilerParams(
-            collective_id=1, has_side_effects=True, vmem_limit_bytes=56 << 20
-        ),
-    )(results, weight, grads)
+            collective_id=1, has_side_effects=True, vmem_limit_bytes=24 << 20
+        ),
+    )(results, grads)
 
 
 def on_device(projected, out_weight, upstream, peak_mask, block_layout):
@@ -573,9 +561,14 @@
     )
     full_weight = lax.all_gather(run_weight, "dp", axis=0, tiled=True)
     results = attention(block_layout[0], qkv, grad_heads)
-    attended, projected_grad, weight_grad = scatter(
-        results, full_weight, run_grads, out_weight.shape[0]
-    )
+    context, projected_grad, weight_grad = scatter(results, run_grads, out_weight.shape[0])
+    attended = lax.dot_general(
+        context.reshape(inner, -1),
+        full_weight,
+        (((0,), (0,)), ((), ())),
+        preferred_element_type=jnp.float32,
+    ).astype(jnp.bfloat16)
+    projected_grad = projected_grad.reshape(3 * inner, -1).T
     return (attended[None], projected_grad[None], weight_grad)
 
 

time: 243 us -> 195 us (0.80)
  Pallas kernels: 199 us -> 167 us
  waiting for transfers between devices: 17.5 us -> 0.02 us
  matrix products: 0 us -> 5.46 us
  local copies, waits for them, and re-layouts: 12.4 us -> 8.09 us
    pallas_call x1, Pallas kernels: 88 us -> 67.6 us  [gather(): pl.pallas_call(gather_kernel, name='gather', out_shape=(jax.ShapeDtypeStr...]
    all_gather x1, waiting for transfers between devices: 17.5 us -> 0.01 us  [on_device(): full_weight = lax.all_gather(run_weight, 'dp', axis=0, tiled=True)]
    pallas_call x1, Pallas kernels: 74 us -> 62.7 us  [scatter(): pl.pallas_call(scatter_kernel, name='scatter', out_shape=(jax.ShapeDtypeS...]
    unnamed x20 -> x16, local copies, waits for them, and re-layouts: 12.4 us -> 6.52 us
    dot_general x0 -> x1, matrix products: none -> 5.46 us  [on_device(): lax.dot_general(context.reshape(inner, -1), full_weight, (((0,), (0,)), (...]
  transfers between devices with their start and end apart: 1 -> 1, of which waited for: 1 -> 0; matrix products, arithmetic and copies ran while one was open for 0% -> 1% of each run, Pallas kernels for 15% -> 51%
where the time goes in v4:
time: 195 us
  Pallas kernels  167 us (86%)
  between operations  14.1 us (7%)
  local copies, waits for them, and re-layouts  8.09 us (4%)
  matrix products  5.46 us (3%)
    pallas_call x1, Pallas kernels, gather(): pl.pallas_call(gather_kernel, name='gather', out_shape=(jax.ShapeDtypeStr...  67.6 us
    pallas_call x1, Pallas kernels, scatter(): pl.pallas_call(scatter_kernel, name='scatter', out_shape=(jax.ShapeDtypeS...  62.7 us
    pallas_call x1, Pallas kernels, attention(): pl.pallas_call(attention_kernel, name='attention', out_shape=jax.ShapeDty...  36.8 us
    unnamed x16, local copies, waits for them, and re-layouts  6.52 us
    dot_general x1, matrix products, on_device(): lax.dot_general(context.reshape(inner, -1), full_weight, (((0,), (0,)), (...  5.46 us
  transfers between devices with their start and end apart: 1, of which 0 were waited for; matrix products, arithmetic and copies ran while one was open for 1% of the time, Pallas kernels for 51%

profile of v4, /device:TPU:1, one launch (start us, length us, event | category | flops | bytes accessed | tf_op | source)
XLA Modules:
  0.0 194.7 jit_solution(13839967631570177847)
XLA Ops:
  7.2 0.0 all-gather.2.cloned.1.call-start
  7.2 0.0 copy-start.2
  7.2 1.4 copy-done.2
  8.6 0.0 copy-start.3
  8.6 1.0 copy-done.3
  9.7 0.0 copy-start.4
  9.7 0.8 copy-done.4
  10.4 0.0 copy-start.5
  10.4 0.7 copy-done.5
  11.1 0.0 copy-start.6
  11.1 67.6 %gather.1 = (bf16[32,3,64,128]{3,2,1,0:T(8,128)(2,1)S(1)}, bf16[32,64,128]{2,1,0:T(8,128)(2,1)S(1)}, bf16[8,128,2048]{2,1,0:T(8,128)(2,1)S(1)}, bf16[256,2048]{1,0:T(8,128)(2,1)}) custom-call(bf16[8,2048]{1,0:T(8,128)(2,1)S(1)} %copy-done.4, bf16[128,6144]{1,0:T(8,128)(2,1)S(1)} %bitcast.15, bf16[128,2048]{1,0:T(8,128)(2,1)S(1)} %bitcast.16, ...), custom_call_target="tpu_custom_call" | custom-call | flops 1073741824 | bytes 16777216 | tf_op jit(solution)/shard_map/gather/pallas_call | solution.py:324
  78.6 0.0 copy-start
  78.6 2.0 %copy-done = bf16[8,128,2048]{2,1,0:T(8,128)(2,1)} copy-done((bf16[8,128,2048]{2,1,0:T(8,128)(2,1)}, bf16[8,128,2048]{2,1,0:T(8,128)(2,1)S(1)}, u32[]{:S(2)}) %copy-start) | copy-done | bytes 4194328
  80.6 0.0 all-gather.2.cloned.1.call-update
  80.6 0.0 copy-done.6
  80.6 0.1 copy.8
  80.7 0.0 copy-start.1
  80.7 36.8 %attention.1.results = bf16[32,4,64,128]{3,2,1,0:T(8,128)(2,1)S(1)} custom-call(s32[32,8]{1,0:T(8,128)S(1)} %bitcast.14, bf16[32,3,64,128]{3,2,1,0:T(8,128)(2,1)S(1)} %get-tuple-element.10.qkv, bf16[32,64,128]{2,1,0:T(8,128)(2,1)S(1)} %get-tuple-element.11.grad), custom_call_target="tpu_custom_call" | custom-call | flops 3221225472 | bytes 4194304 | tf_op jit(solution)/shard_map/attention/pallas_call | solution.py:83
  117.5 0.0 copy-done.1
  117.5 62.7 %scatter.1 = (bf16[32,64,128]{2,1,0:T(8,128)(2,1)S(1)}, bf16[3,32,64,128]{3,2,1,0:T(8,128)(2,1)S(1)}, f32[8,2048]{1,0:T(8,128)S(1)}) custom-call(bf16[32,4,64,128]{3,2,1,0:T(8,128)(2,1)S(1)} %attention.1.results, bf16[8,128,2048]{2,1,0:T(8,128)(2,1)S(1)} %copy-done.1), custom_call_target="tpu_custom_call" | custom-call | flops 1073741824 | bytes 20971520 | tf_op jit(solution)/shard_map/scatter/pallas_call | solution.py:527
  180.2 1.6 copy.9
  181.8 0.0 all-gather.2.cloned.1.call-done
  181.8 5.5 %fusion = bf16[1,128,2048]{2,1,0:T(8,128)(2,1)} fusion(bf16[2048,128]{1,0:T(8,128)(2,1)S(1)} %bitcast.12, bf16[2048,2048]{1,0:T(8,128)(2,1)} %all-gather.2.cloned.1.call-done), kind=kOutput, calls=%fused_computation.1 | convolution fusion | flops 1074003968 | bytes 9437184 | tf_op jit(solution)/shard_map/dot_general | solution.py:565
  187.2 0.6 copy.11
Async XLA Ops:
  7.2 174.6 %all-gather.2.cloned.1.call-start = ((), (), s32[]{:S(2)}) async-start(), calls=%async_computation | async-start | bytes 9437184 | tf_op jit(solution)/shard_map/all_gather | solution.py:562
  7.2 1.4 copy-start.2
  8.6 1.0 copy-start.3
  9.7 0.8 copy-start.4
  10.4 0.7 copy-start.5
  11.1 69.6 %copy-start.6 = (s32[1,32,8]{1,2,0:T(8,128)S(1)}, s32[1,32,8]{1,2,0:T(8,128)}, u32[]{:S(2)}) copy-start(s32[1,32,8]{1,2,0:T(8,128)} %param.9) | copy-start | bytes 3076
  78.6 2.0 %copy-start = (bf16[8,128,2048]{2,1,0:T(8,128)(2,1)}, bf16[8,128,2048]{2,1,0:T(8,128)(2,1)S(1)}, u32[]{:S(2)}) copy-start(bf16[8,128,2048]{2,1,0:T(8,128)(2,1)S(1)} %get-tuple-element.12.grads) | copy-start | bytes 12582916
  80.7 36.8 %copy-start.1 = (bf16[8,128,2048]{2,1,0:T(8,128)(2,1)S(1)}, bf16[8,128,2048]{2,1,0:T(8,128)(2,1)}, u32[]{:S(2)}) copy-start(bf16[8,128,2048]{2,1,0:T(8,128)(2,1)} %copy-done) | copy-start | bytes 12582916
Sparse Core Ops, SparseCore 0:
  80.7 50.1 all-gather.1

commit v5 on v4

--- a/solution.py
+++ b/solution.py
@@ -13,66 +13,84 @@
     blocks, _, head, length = qkv.shape
     picks = layout.shape[1]
     pair = 2 * head
+    eighths = length // 8
 
     def prepare(b, carry):
         kvn[b] = qkv[b, 1:3].reshape(pair, length).T
         acc[b] = jnp.zeros((length, pair), jnp.float32)
         return carry
 
-    lax.fori_loop(0, blocks, prepare, 0)
+    lax.fori_loop(0, blocks, prepare, 0, unroll=4)
     low = lax.broadcasted_iota(jnp.int32, (length, pair), 1) < head
 
-    def row_block(r, carry):
+    def picked(r):
+        return [layout[r, j] for j in range(picks)]
+
+    def scores_of(r, slot):
         q = qkv[r, 0] * jnp.bfloat16(SCALE)
         g = grad[r]
         none = jnp.zeros_like(q)
-        turned = jnp.concatenate([q, g], 0).T
-        into_scores = jnp.concatenate(
-            [jnp.concatenate([q, none], 1), jnp.concatenate([none, g], 1)], 0
-        )
-        into_keys = jnp.concatenate(
-            [jnp.where(low, turned, 0), jnp.where(low, 0, turned)], 0
-        )
-        at = [layout[r, j] for j in range(picks)]
+        into = jnp.concatenate([jnp.concatenate([q, none], 1), jnp.concatenate([none, g], 1)], 0)
         top = None
-        for j in range(picks):
-            both = jnp.dot(kvn[at[j]], into_scores, preferred_element_type=jnp.float32)
-            scores[j] = both
-            part = jnp.max(both[:, :length].reshape(length // 8, 8, length), axis=0)
+        for j, b in enumerate(picked(r)):
+            both = jnp.dot(kvn[b], into, preferred_element_type=jnp.float32)
+            scores[slot, j] = both
+            part = jnp.max(both[:, :length].reshape(eighths, 8, length), axis=0)
             top = part if top is None else jnp.maximum(top, part)
-        top = jnp.max(top, axis=0, keepdims=True)
+        return jnp.max(top, axis=0, keepdims=True)
+
+    def probs_of(slot, top):
         total = jnp.zeros((8, length), jnp.float32)
         delta = jnp.zeros((8, length), jnp.float32)
         for j in range(picks):
-            e = jnp.exp(scores[j, :, :length] - top)
-            scores[j, :, :length] = e
-            total += jnp.sum(e.reshape(length // 8, 8, length), axis=0)
-            delta += jnp.sum((e * scores[j, :, length:]).reshape(length // 8, 8, length), axis=0)
+            e = jnp.exp(scores[slot, j, :, :length] - top)
+            scores[slot, j, :, :length] = e
+            total += jnp.sum(e.reshape(eighths, 8, length), axis=0)
+            delta += jnp.sum((e * scores[slot, j, :, length:]).reshape(eighths, 8, length), axis=0)
         inverse = 1.0 / jnp.sum(total, axis=0, keepdims=True)
         delta = jnp.sum(delta, axis=0, keepdims=True) * inverse
         for j in range(picks):
-            p = scores[j, :, :length] * inverse
-            d = p * (scores[j, :, length:] - delta)
+            p = scores[slot, j, :, :length] * inverse
+            d = p * (scores[slot, j, :, length:] - delta)
             rows = pl.ds(j * length, length)
-            probs[rows, :length] = d.astype(jnp.bfloat16)
-            probs[rows, length:] = p.astype(jnp.bfloat16)
-        kvt = jnp.concatenate([qkv[at[j], 1:3].reshape(pair, length) for j in range(picks)], 1)
-        both = jnp.dot(kvt, probs[...], preferred_element_type=jnp.float32)
+            probs[slot, rows, :length] = d.astype(jnp.bfloat16)
+            probs[slot, rows, length:] = p.astype(jnp.bfloat16)
+
+    def results_of(r, slot):
+        at = picked(r)
+        kvt = jnp.concatenate([qkv[b, 1:3].reshape(pair, length) for b in at], 1)
+        both = jnp.dot(kvt, probs[slot], preferred_element_type=jnp.float32)
         out[r, 0] = both[head:, length:].astype(jnp.bfloat16)
         out[r, 1] = (both[:head, :length] * SCALE).astype(jnp.bfloat16)
-        for j in range(picks):
-            acc[at[j]] += jnp.dot(
-                probs[pl.ds(j * length, length), :], into_keys, preferred_element_type=jnp.float32
+        turned = jnp.concatenate([qkv[r, 0] * jnp.bfloat16(SCALE), grad[r]], 0).T
+        into = jnp.concatenate([jnp.where(low, turned, 0), jnp.where(low, 0, turned)], 0)
+        for j, b in enumerate(at):
+            acc[b] += jnp.dot(
+                probs[slot, pl.ds(j * length, length), :], into, preferred_element_type=jnp.float32
             )
-        return carry
-
-    lax.fori_loop(0, blocks, row_block, 0)
+
+    probs_of(0, scores_of(0, 0))
+
+    def two_rows(i, top):
+        r = 2 * i
+        later = scores_of(r + 2, 0)
+        results_of(r, 0)
+        probs_of(1, top)
+        last = scores_of(r + 3, 1)
+        results_of(r + 1, 1)
+        probs_of(0, later)
+        return last
+
+    top = lax.fori_loop(0, blocks // 2 - 1, two_rows, scores_of(1, 1))
+    results_of(blocks - 2, 0)
+    probs_of(1, top)
+    results_of(blocks - 1, 1)
 
     def finish(b, carry):
         out[b, 2:4] = acc[b].T.astype(jnp.bfloat16).reshape(2, head, length)
         return carry
 
-    lax.fori_loop(0, blocks, finish, 0)
+    lax.fori_loop(0, blocks, finish, 0, unroll=4)
 
 
 def attention(layout, qkv, grad):
@@ -89,8 +107,8 @@
         scratch_shapes=[
             pltpu.VMEM((blocks, length, 2 * head), jnp.bfloat16),
             pltpu.VMEM((blocks, length, 2 * head), jnp.float32),
-            pltpu.VMEM((keys, 2 * length), jnp.bfloat16),
-            pltpu.VMEM((picks, length, 2 * length), jnp.float32),
+            pltpu.VMEM((2, keys, 2 * length), jnp.bfloat16),
+            pltpu.VMEM((2, picks, length, 2 * length), jnp.float32),
         ],
         cost_estimate=pl.CostEstimate(
             flops=12 * blocks * length * keys * head,

time: 195 us -> 184 us (0.944)
  Pallas kernels: 167 us -> 155 us
    pallas_call x1, Pallas kernels: 36.8 us -> 20.9 us  [attention(): pl.pallas_call(attention_kernel, name='attention', out_shape=jax.ShapeDty...]
    pallas_call x1, Pallas kernels: 62.7 us -> 66.5 us  [scatter(): pl.pallas_call(scatter_kernel, name='scatter', out_shape=(jax.ShapeDtypeS...]
  transfers between devices with their start and end apart: 1 -> 1, of which waited for: 0 -> 0; matrix products, arithmetic and copies ran while one was open for 1% -> 1% of each run, Pallas kernels for 51% -> 48%
where the time goes in v5:
time: 184 us; the launch traced here: 183 us
  Pallas kernels  155 us (84%)
  between operations  14.1 us (8%)
  local copies, waits for them, and re-layouts  8.09 us (4%)
  matrix products  5.46 us (3%)
    pallas_call x1, Pallas kernels, gather(): pl.pallas_call(gather_kernel, name='gather', out_shape=(jax.ShapeDtypeStr...  67.6 us
    pallas_call x1, Pallas kernels, scatter(): pl.pallas_call(scatter_kernel, name='scatter', out_shape=(jax.ShapeDtypeS...  66.5 us
    pallas_call x1, Pallas kernels, attention(): pl.pallas_call(attention_kernel, name='attention', out_shape=jax.ShapeDty...  20.9 us
    unnamed x16, local copies, waits for them, and re-layouts  6.52 us
    dot_general x1, matrix products, on_device(): lax.dot_general(context.reshape(inner, -1), full_weight, (((0,), (0,)), (...  5.46 us
  transfers between devices with their start and end apart: 1, of which 0 were waited for; matrix products, arithmetic and copies ran while one was open for 1% of the time, Pallas kernels for 48%

profile of v5, /device:TPU:1, one launch (start us, length us, event | category | flops | bytes accessed | tf_op | source)
XLA Modules:
  0.0 182.7 jit_solution(198139396657896766)
XLA Ops:
  7.2 0.0 all-gather.2.cloned.1.call-start
  7.2 0.0 copy-start.2
  7.2 1.4 copy-done.2
  8.6 0.0 copy-start.3
  8.6 1.0 copy-done.3
  9.7 0.0 copy-start.4
  9.7 0.8 copy-done.4
  10.4 0.0 copy-start.5
  10.4 0.7 copy-done.5
  11.1 0.0 copy-start.6
  11.1 67.6 %gather.1 = (bf16[32,3,64,128]{3,2,1,0:T(8,128)(2,1)S(1)}, bf16[32,64,128]{2,1,0:T(8,128)(2,1)S(1)}, bf16[8,128,2048]{2,1,0:T(8,128)(2,1)S(1)}, bf16[256,2048]{1,0:T(8,128)(2,1)}) custom-call(bf16[8,2048]{1,0:T(8,128)(2,1)S(1)} %copy-done.4, bf16[128,6144]{1,0:T(8,128)(2,1)S(1)} %bitcast.15, bf16[128,2048]{1,0:T(8,128)(2,1)S(1)} %bitcast.16, ...), custom_call_target="tpu_custom_call" | custom-call | flops 1073741824 | bytes 16777216 | tf_op jit(solution)/shard_map/gather/pallas_call | solution.py:342
  78.6 0.0 copy-start
  78.6 2.0 %copy-done = bf16[8,128,2048]{2,1,0:T(8,128)(2,1)} copy-done((bf16[8,128,2048]{2,1,0:T(8,128)(2,1)}, bf16[8,128,2048]{2,1,0:T(8,128)(2,1)S(1)}, u32[]{:S(2)}) %copy-start) | copy-done | bytes 4194328
  80.6 0.0 all-gather.2.cloned.1.call-update
  80.6 0.0 copy-done.6
  80.6 0.1 copy.8
  80.7 0.0 copy-start.1
  80.7 20.9 %attention.1.results = bf16[32,4,64,128]{3,2,1,0:T(8,128)(2,1)S(1)} custom-call(s32[32,8]{1,0:T(8,128)S(1)} %bitcast.14, bf16[32,3,64,128]{3,2,1,0:T(8,128)(2,1)S(1)} %get-tuple-element.10.qkv, bf16[32,64,128]{2,1,0:T(8,128)(2,1)S(1)} %get-tuple-element.11.grad), custom_call_target="tpu_custom_call" | custom-call | flops 3221225472 | bytes 4194304 | tf_op jit(solution)/shard_map/attention/pallas_call | solution.py:101
  101.6 0.0 copy-done.1
  101.7 66.5 %scatter.1 = (bf16[32,64,128]{2,1,0:T(8,128)(2,1)S(1)}, bf16[3,32,64,128]{3,2,1,0:T(8,128)(2,1)S(1)}, f32[8,2048]{1,0:T(8,128)S(1)}) custom-call(bf16[32,4,64,128]{3,2,1,0:T(8,128)(2,1)S(1)} %attention.1.results, bf16[8,128,2048]{2,1,0:T(8,128)(2,1)S(1)} %copy-done.1), custom_call_target="tpu_custom_call" | custom-call | flops 1073741824 | bytes 20971520 | tf_op jit(solution)/shard_map/scatter/pallas_call | solution.py:545
  168.1 1.6 copy.9
  169.7 0.0 all-gather.2.cloned.1.call-done
  169.7 5.5 %fusion = bf16[1,128,2048]{2,1,0:T(8,128)(2,1)} fusion(bf16[2048,128]{1,0:T(8,128)(2,1)S(1)} %bitcast.12, bf16[2048,2048]{1,0:T(8,128)(2,1)} %all-gather.2.cloned.1.call-done), kind=kOutput, calls=%fused_computation.1 | convolution fusion | flops 1074003968 | bytes 9437184 | tf_op jit(solution)/shard_map/dot_general | solution.py:583
  175.2 0.6 copy.11
Async XLA Ops:
  7.2 162.6 %all-gather.2.cloned.1.call-start = ((), (), s32[]{:S(2)}) async-start(), calls=%async_computation | async-start | bytes 9437184 | tf_op jit(solution)/shard_map/all_gather | solution.py:580
  7.2 1.4 copy-start.2
  8.6 1.0 copy-start.3
  9.7 0.8 copy-start.4
  10.4 0.7 copy-start.5
  11.1 69.6 %copy-start.6 = (s32[1,32,8]{1,2,0:T(8,128)S(1)}, s32[1,32,8]{1,2,0:T(8,128)}, u32[]{:S(2)}) copy-start(s32[1,32,8]{1,2,0:T(8,128)} %param.9) | copy-start | bytes 3076
  78.6 2.0 %copy-start = (bf16[8,128,2048]{2,1,0:T(8,128)(2,1)}, bf16[8,128,2048]{2,1,0:T(8,128)(2,1)S(1)}, u32[]{:S(2)}) copy-start(bf16[8,128,2048]{2,1,0:T(8,128)(2,1)S(1)} %get-tuple-element.12.grads) | copy-start | bytes 12582916
  80.7 20.9 %copy-start.1 = (bf16[8,128,2048]{2,1,0:T(8,128)(2,1)S(1)}, bf16[8,128,2048]{2,1,0:T(8,128)(2,1)}, u32[]{:S(2)}) copy-start(bf16[8,128,2048]{2,1,0:T(8,128)(2,1)} %copy-done) | copy-start | bytes 12582916
Sparse Core Ops, SparseCore 0:
  80.7 54.6 all-gather.1

commit v6 on v4

v6 whole, which is shorter than its diff:
```python
import jax
import jax.numpy as jnp
from jax import lax
from jax.experimental import pallas as pl
from jax.experimental.pallas import tpu as pltpu
from jax.sharding import PartitionSpec as P

HS = 64
SCALE = 0.125


MESH = pl.DeviceIdType.MESH


def place():
    d, s = lax.axis_index("dp"), lax.axis_index("seq")
    return d, d // 2, d % 2, s, s // 4, s % 4


def shifted(z, y, k):
    along, across = k // 4, k % 4
    along = 4 + (1 - along % 2 * 2) * ((along + 1) // 2)
    across = 2 + (1 - across % 2 * 2) * ((across + 1) // 2)
    return (z + along) % 8 * 4 + (y + across) % 4


def layer_kernel(
    layout, where, weight, rows_in, upstream_in, mask_in, attended, pieces, weight_grad,
    qkv, grad, grads, run_weight, rows, upstream, mask, turned, sent, mixed, full_weight,
    kvn, parts, probs, scores, out, context, swapped, partial, across, along,
    in_sem, w_send, w_recv, m_send, m_recv, q_send, q_recv, x_send, x_recv, g_send, g_recv,
    f_send, f_recv, c_send, c_recv, b_send, b_recv, k_send, k_recv,
    s_send, s_recv, a_send, a_recv, l_send, l_recv,
):
    d, x, core, s, z, y = place()
    tokens, model = upstream.shape
    heads, _, head, _ = qkv.shape
    seq, runs, depth = heads, grads.shape[0], weight.shape[0]
    group = heads // runs
    share = group * head
    other = d + 1 - 2 * core

    def to(dp, at):
        return {"device_id": (dp, at), "device_id_type": MESH}

    def weight_rows(at):
        return run_weight.at[pl.ds(pl.multiple_of(at * depth, depth), depth)]

    loads = [
        pltpu.make_async_copy(upstream_in, upstream, in_sem.at[0]),
        pltpu.make_async_copy(mask_in, mask, in_sem.at[1]),
        pltpu.make_async_copy(rows_in, rows, in_sem.at[2]),
        pltpu.make_async_copy(weight, weight_rows(s), in_sem.at[3]),
    ]
    for load in loads:
        load.start()
    barrier = pltpu.get_barrier_semaphore()

    def greet_seq(k, carry):
        pl.semaphore_signal(barrier, inc=1, **to(d, shifted(z, y, k)))
        return carry

    def greet_dp(k, carry):
        pl.semaphore_signal(barrier, inc=1, **to((d + k) % runs, s))
        return carry

    lax.fori_loop(0, seq - 1, greet_seq, 0)
    lax.fori_loop(1, runs, greet_dp, 0)
    loads[0].wait()
    loads[1].wait()
    column = jnp.broadcast_to(mask[...].astype(jnp.float32), (tokens, tokens)).T.astype(jnp.bfloat16)
    for i in range(model // tokens):
        part = slice(i * tokens, (i + 1) * tokens)
        grads[d, :, part] = upstream[:, part] * column

    def turn(pair, carry):
        for c in range(3):
            at = pl.multiple_of(c * (heads * head) + pair * 2 * head, 2 * head)
            both = rows[:, pl.ds(at, 2 * head)].T
            turned[2 * pair, c] = both[:head]
            turned[2 * pair + 1, c] = both[head:]
        return carry

    loads[2].wait()
    lax.fori_loop(0, heads // 2, turn, 0)
    loads[3].wait()

    pl.semaphore_wait(barrier, seq - 1 + runs - 1)

    def weight_copy(at, k, peer):
        return pltpu.make_async_remote_copy(
            weight_rows(at), weight_rows(at), w_send.at[k], w_recv.at[at], **to(d, peer)
        )

    def weight_z(k, carry):
        weight_copy(s, k, (z + k) % 8 * 4 + y).start()
        return carry

    lax.fori_loop(1, 8, weight_z, 0)

    def grad_copy(run, k, peer):
        return pltpu.make_async_remote_copy(
            grads.at[run], grads.at[run], m_send.at[k], m_recv.at[run], **to(peer, s)
        )

    def chip(k):
        return (x + k) % 4 * 2

    def grads_x(k, carry):
        grad_copy(d, k, chip(k) + core).start()
        return carry

    lax.fori_loop(1, 4, grads_x, 0)
    grad_copy(d, 0, d + 1 - 2 * core).start()

    def qkv_copy(k):
        peer = shifted(z, y, k)
        return pltpu.make_async_remote_copy(
            turned.at[peer], qkv.at[s], q_send.at[k], q_recv.at[k], **to(d, peer)
        )

    def send_qkv(k, carry):
        qkv_copy(k).start()
        return carry

    lax.fori_loop(0, seq - 1, send_qkv, 0)
    qkv[s] = turned[s]

    def weight_y(k, carry):
        at = (z + k) % 8 * 4 + y

        @pl.when(k > 0)
        def _():
            weight_copy(at, 0, s).wait_recv()

        for i in range(1, 4):
            weight_copy(at, 8 * i + k, z * 4 + (y + i) % 4).start()
        return carry

    lax.fori_loop(0, 8, weight_y, 0)

    def weight_wait(k, carry):
        for i in range(1, 4):
            weight_copy(k * 4 + (y + i) % 4, 0, s).wait_recv()
        return carry

    lax.fori_loop(0, 8, weight_wait, 0)

    def sent_copy(run, source):
        return pltpu.make_async_remote_copy(
            sent.at[run], mixed.at[source], x_send.at[run], x_recv.at[source], **to(run, s)
        )

    def one_run(run):
        value = lax.dot_general(
            run_weight[...], grads[run], (((1,), (1,)), ((), ())), preferred_element_type=jnp.float32
        )
        sent[run] = value.astype(jnp.bfloat16).reshape(heads // runs, head, tokens)

        @pl.when(run != d)
        def _():
            sent_copy(run, d).start()

    def runs_near(k, carry):
        run = chip(k) + core

        @pl.when(k > 0)
        def _():
            grad_copy(run, 0, d).wait_recv()
            grad_copy(run, 3 + k, d + 1 - 2 * core).start()

        one_run(run)
        return carry

    lax.fori_loop(0, 4, runs_near, 0)

    def runs_other(k, carry):
        run = chip(k) + 1 - core
        grad_copy(run, 0, d).wait_recv()
        one_run(run)
        return carry

    lax.fori_loop(0, 4, runs_other, 0)

    mixed[d] = sent[d]

    def full_copy(run, k, peer):
        source = run_weight if run is d else full_weight.at[run]
        return pltpu.make_async_remote_copy(
            source, full_weight.at[run], f_send.at[k], f_recv.at[run], **to(peer, s)
        )

    def full_x(k, carry):
        full_copy(d, k, chip(k) + core).start()
        return carry

    lax.fori_loop(1, 4, full_x, 0)
    full_copy(d, 0, other).start()

    def wait_mixed(k, carry):
        sent_copy(d, (d + k) % runs).wait_recv()
        return carry

    lax.fori_loop(1, runs, wait_mixed, 0)

    def head_copy(k):
        peer = shifted(z, y, k)
        return pltpu.make_async_remote_copy(
            mixed.at[peer // group, peer % group], grad.at[s], g_send.at[k], g_recv.at[k], **to(d, peer)
        )

    def send_head(k, carry):
        head_copy(k).start()
        return carry

    lax.fori_loop(0, seq - 1, send_head, 0)
    grad[s] = mixed[s // (heads // runs), s % (heads // runs)]

    def arrive_qkv(k, carry):
        qkv_copy(k).wait_recv()
        return carry

    lax.fori_loop(0, seq - 1, arrive_qkv, 0)

    blocks, length = heads, tokens
    picks = layout.shape[1]
    pair = 2 * head
    eighths = length // 8

    def prepare(b, carry):
        kvn[b] = qkv[b, 1:3].reshape(pair, length).T
        return carry

    lax.fori_loop(0, blocks, prepare, 0, unroll=4)
    parts[blocks * picks] = jnp.zeros((length, pair), jnp.float32)

    def arrive_grad(k, carry):
        head_copy(k).wait_recv()
        return carry

    lax.fori_loop(0, seq - 1, arrive_grad, 0)
    low = lax.broadcasted_iota(jnp.int32, (length, pair), 1) < head

    def picked(r):
        return [layout[r, j] for j in range(picks)]

    def scores_of(r, slot):
        q = qkv[r, 0] * jnp.bfloat16(SCALE)
        g = grad[r]
        none = jnp.zeros_like(q)
        into = jnp.concatenate([jnp.concatenate([q, none], 1), jnp.concatenate([none, g], 1)], 0)
        top = None
        for j, b in enumerate(picked(r)):
            both = jnp.dot(kvn[b], into, preferred_element_type=jnp.float32)
            scores[slot, j] = both
            part = jnp.max(both[:, :length].reshape(eighths, 8, length), axis=0)
            top = part if top is None else jnp.maximum(top, part)
        return jnp.max(top, axis=0, keepdims=True)

    def probs_of(slot, top):
        total = jnp.zeros((8, length), jnp.float32)
        delta = jnp.zeros((8, length), jnp.float32)
        for j in range(picks):
            e = jnp.exp(scores[slot, j, :, :length] - top)
            scores[slot, j, :, :length] = e
            total += jnp.sum(e.reshape(eighths, 8, length), axis=0)
            delta += jnp.sum((e * scores[slot, j, :, length:]).reshape(eighths, 8, length), axis=0)
        inverse = 1.0 / jnp.sum(total, axis=0, keepdims=True)
        delta = jnp.sum(delta, axis=0, keepdims=True) * inverse
        for j in range(picks):
            p = scores[slot, j, :, :length] * inverse
            d = p * (scores[slot, j, :, length:] - delta)
            rows = pl.ds(j * length, length)
            probs[slot, rows, :length] = d.astype(jnp.bfloat16)
            probs[slot, rows, length:] = p.astype(jnp.bfloat16)

    def results_of(r, slot):
        at = picked(r)
        kvt = jnp.concatenate([qkv[b, 1:3].reshape(pair, length) for b in at], 1)
        both = jnp.dot(kvt, probs[slot], preferred_element_type=jnp.float32)
        out[r, 0] = both[head:, length:].astype(jnp.bfloat16)
        out[r, 1] = (both[:head, :length] * SCALE).astype(jnp.bfloat16)
        turned = jnp.concatenate([qkv[r, 0] * jnp.bfloat16(SCALE), grad[r]], 0).T
        into = jnp.concatenate([jnp.where(low, turned, 0), jnp.where(low, 0, turned)], 0)
        for j in range(picks):
            parts[r * picks + j] = jnp.dot(
                probs[slot, pl.ds(j * length, length), :], into, preferred_element_type=jnp.float32
            )

    def context_copy(k):
        peer = shifted(z, y, k)
        return pltpu.make_async_remote_copy(
            out.at[peer, 0], context.at[s], c_send.at[k], c_recv.at[k], **to(d, peer)
        )

    def query_copy(k):
        peer = shifted(z, y, k)
        return pltpu.make_async_remote_copy(
            out.at[peer, 1], pieces.at[0, s], b_send.at[k], b_recv.at[k], **to(d, peer)
        )

    def key_copy(k):
        peer = shifted(z, y, k)
        return pltpu.make_async_remote_copy(
            out.at[peer, pl.ds(2, 2)], pieces.at[pl.ds(1, 2), s], k_send.at[k], k_recv.at[k], **to(d, peer)
        )

    def row(k):
        return shifted(z, y, k)

    def give(k, slot):
        results_of(row(k), slot)
        context_copy(k).start()
        query_copy(k).start()

    probs_of(0, scores_of(row(0), 0))

    def two_rows(i, top):
        k = 2 * i
        later = scores_of(row(k + 2), 0)
        give(k, 0)
        probs_of(1, top)
        last = scores_of(row(k + 3), 1)
        give(k + 1, 1)
        probs_of(0, later)
        return last

    top = lax.fori_loop(0, blocks // 2 - 1, two_rows, scores_of(row(1), 1))
    give(blocks - 2, 0)
    probs_of(1, top)
    results_of(s, 1)
    context[s] = out[s, 0]
    pieces[0, s] = out[s, 1]

    def wait_context(k, carry):
        context_copy(k).wait_recv()
        return carry

    lax.fori_loop(0, seq - 1, wait_context, 0)

    def swap_copy(k):
        peer = (d + k) % runs
        return pltpu.make_async_remote_copy(
            context.at[pl.ds(peer * group, group)], swapped.at[d], s_send.at[k], s_recv.at[k], **to(peer, s)
        )

    def send_swap(k, carry):
        swap_copy(k).start()
        return carry

    lax.fori_loop(1, runs, send_swap, 0)
    swapped[d] = context[pl.ds(d * group, group)]

    def keys_of(u):
        total = parts[where[u, 0]]
        for r in range(1, blocks):
            total += parts[where[u, r]]
        out[u, 2:4] = total.T.astype(jnp.bfloat16).reshape(2, head, length)

    def give_keys(k, carry):
        keys_of(row(k))
        key_copy(k).start()
        return carry

    lax.fori_loop(0, seq - 1, give_keys, 0)
    keys_of(s)
    pieces[1:3, s] = out[s, 2:4]

    def wait_swap(k, carry):
        swap_copy(k).wait_recv()
        return carry

    lax.fori_loop(1, runs, wait_swap, 0)

    wide = 512

    def multiply(i, carry):
        at = pl.ds(pl.multiple_of(i * wide, wide), wide)
        left = jnp.concatenate([swapped[r].reshape(share, tokens) for r in range(runs)], 1)
        right = grads[:, :, at].reshape(runs * tokens, wide)
        total = jnp.dot(left, right, preferred_element_type=jnp.float32).astype(jnp.bfloat16)
        for k in range(heads):
            partial[k % 4, k // 4, :, at] = total[k * depth : (k + 1) * depth]
        return carry

    lax.fori_loop(0, model // wide, multiply, 0)

    def across_copy(k):
        peer = (y + k) % 4
        return pltpu.make_async_remote_copy(
            partial.at[peer], across.at[k], a_send.at[k], a_recv.at[k], **to(d, z * 4 + peer)
        )

    for k in range(1, 4):
        across_copy(k).start()

    def attend(run, rows):
        left = context[pl.ds(run * group, group)].reshape(share, tokens).T
        return jnp.dot(left, rows, preferred_element_type=jnp.float32)

    def full_near(k, carry):
        run = chip(k) + core
        full_copy(run, 0, d).wait_recv()
        full_copy(run, 3 + k, other).start()
        attended[...] += attend(run, full_weight[run])
        return carry

    def full_other(k, carry):
        run = chip(k) + 1 - core
        full_copy(run, 0, d).wait_recv()
        attended[...] += attend(run, full_weight[run])
        return carry

    attended[...] = attend(d, run_weight[...])
    lax.fori_loop(1, 4, full_near, 0)

    for k in range(1, 4):
        across_copy(k).wait_recv()

    def add_across(k, carry):
        total = partial[y, k].astype(jnp.float32)
        for i in range(1, 4):
            total += across[i, k].astype(jnp.float32)
        across[0, k] = total.astype(jnp.bfloat16)
        return carry

    def along_copy(k):
        peer = (z + k) % 8
        return pltpu.make_async_remote_copy(
            across.at[0, peer], along.at[k], l_send.at[k], l_recv.at[k], **to(d, peer * 4 + y)
        )

    def send_along(k, carry):
        along_copy(k).start()
        return carry

    lax.fori_loop(0, 8, add_across, 0)
    lax.fori_loop(1, 8, send_along, 0)
    lax.fori_loop(0, 4, full_other, 0)

    def wait_along(k, carry):
        along_copy(k).wait_recv()
        return carry

    lax.fori_loop(1, 8, wait_along, 0)
    total = across[0, z].astype(jnp.float32)
    for k in range(1, 8):
        total += along[k].astype(jnp.float32)
    weight_grad[...] = total

    def finish_seq(k, carry):
        qkv_copy(k).wait_send()
        head_copy(k).wait_send()
        context_copy(k).wait_send()
        query_copy(k).wait()
        key_copy(k).wait()
        return carry

    lax.fori_loop(0, seq - 1, finish_seq, 0)

    def finish_swap(k, carry):
        swap_copy(k).wait_send()
        return carry

    def finish_along(k, carry):
        along_copy(k).wait_send()
        return carry

    lax.fori_loop(1, runs, finish_swap, 0)
    for k in range(1, 4):
        across_copy(k).wait_send()
    lax.fori_loop(1, 8, finish_along, 0)

    def finish_sent(k, carry):
        sent_copy((d + k) % runs, d).wait_send()
        return carry

    lax.fori_loop(1, runs, finish_sent, 0)

    def finish_weight(k, carry):
        weight_copy(s, k, s).wait_send()
        return carry

    lax.fori_loop(1, 32, finish_weight, 0)

    def finish_grads(k, carry):
        grad_copy(d, k, d).wait_send()
        return carry

    lax.fori_loop(0, 7, finish_grads, 0)

    def finish_full(k, carry):
        full_copy(d, k, other).wait_send()
        return carry

    lax.fori_loop(0, 7, finish_full, 0)


def layer(layout, where, weight, rows, upstream, mask, runs):
    tokens, model = upstream.shape
    heads, picks = layout.shape
    depth = weight.shape[0]
    group = heads // runs
    bf16, f32, dma = jnp.bfloat16, jnp.float32, pltpu.SemaphoreType.DMA
    vmem, smem = pl.BlockSpec(memory_space=pltpu.VMEM), pl.BlockSpec(memory_space=pltpu.SMEM)
    each, some = dma((heads,)), dma((8,))
    return pl.pallas_call(
        layer_kernel,
        name="layer",
        out_shape=(
            jax.ShapeDtypeStruct((tokens, model), f32),
            jax.ShapeDtypeStruct((3, heads, HS, tokens), bf16),
            jax.ShapeDtypeStruct((depth, model), f32),
        ),
        in_specs=[smem, smem] + [pl.BlockSpec(memory_space=pltpu.HBM)] * 4,
        out_specs=(vmem,) * 3,
        scratch_shapes=[
            pltpu.VMEM((heads, 3, HS, tokens), bf16),
            pltpu.VMEM((heads, HS, tokens), bf16),
            pltpu.VMEM((runs, tokens, model), bf16),
            pltpu.VMEM((heads * depth, model), bf16),
            pltpu.VMEM(rows.shape, bf16),
            pltpu.VMEM(upstream.shape, bf16),
            pltpu.VMEM(mask.shape, jnp.int32),
            pltpu.VMEM((heads, 3, HS, tokens), bf16),
            pltpu.VMEM((runs, group, HS, tokens), bf16),
            pltpu.VMEM((runs, group, HS, tokens), bf16),
            pltpu.VMEM((runs, heads * depth, model), bf16),
            pltpu.VMEM((heads, tokens, 2 * HS), bf16),
            pltpu.VMEM((heads * picks + 1, tokens, 2 * HS), f32),
            pltpu.VMEM((2, picks * tokens, 2 * tokens), bf16),
            pltpu.VMEM((2, picks, tokens, 2 * tokens), f32),
            pltpu.VMEM((heads, 4, HS, tokens), bf16),
            pltpu.VMEM((heads, HS, tokens), bf16),
            pltpu.VMEM((runs, group, HS, tokens), bf16),
            pltpu.VMEM((4, 8, depth, model), bf16),
            pltpu.VMEM((4, 8, depth, model), bf16),
            pltpu.VMEM((8, depth, model), bf16),
            dma((4,)), each, each, some, some, each, each, some, some, each, each,
            some, some, each, each, each, each, each, each,
            some, some, dma((4,)), dma((4,)), some, some,
        ],
        cost_estimate=pl.CostEstimate(
            flops=20 * heads * tokens * picks * tokens * HS, bytes_accessed=16 << 20, transcendentals=0
        ),
        compiler_params=pltpu.CompilerParams(
            collective_id=0, has_side_effects=True, vmem_limit_bytes=58 << 20
        ),
    )(layout, where, weight, rows, upstream, mask)


def on_device(projected, out_weight, upstream, peak_mask, block_layout):
    inner = projected.shape[2] // 3
    layout = block_layout[0]
    blocks, picks = layout.shape
    index = jnp.arange(blocks * picks, dtype=jnp.int32).reshape(1, blocks, picks)
    same = layout[None] == jnp.arange(blocks, dtype=jnp.int32)[:, None, None]
    where = jnp.min(jnp.where(same, index, blocks * picks), axis=2)
    attended, projected_grad, weight_grad = layer(
        layout, where, out_weight, projected[0], upstream[0], peak_mask, lax.axis_size("dp")
    )
    projected_grad = projected_grad.reshape(3 * inner, -1).T
    return (attended.astype(jnp.bfloat16)[None], projected_grad[None], weight_grad)


def solution(mesh):
    in_specs = (
        P("dp", "seq", None),
        P(("dp", "seq"), None),
        P("dp", "seq", None),
        P("dp", "seq"),
        P("seq", None, None),
    )
    out_specs = (P("dp", "seq", None), P("dp", "seq", None), P(("dp", "seq"), None))
    return jax.shard_map(
        on_device, mesh=mesh, in_specs=in_specs, out_specs=out_specs, check_vma=False
    )
```

time: 195 us -> 154 us (0.79)
  the two profiles are of different devices: /device:TPU:1 before, /device:TPU:38 now
where the time goes in v6:
time: 154 us; the launch traced here: 153 us
  Pallas kernels  146 us (95%)
  other arithmetic  3.57 us (2%)
  local copies, waits for them, and re-layouts  3.56 us (2%)
    pallas_call x1, Pallas kernels, layer(): pl.pallas_call(layer_kernel, name='layer', out_shape=(jax.ShapeDtypeStruc...  146 us

profile of v6, /device:TPU:38, one launch (start us, length us, event | category | flops | bytes accessed | tf_op | source)
XLA Modules:
  0.0 153.3 jit_solution(10369723004575750485)
XLA Ops:
  0.6 1.4 select_reduce_fusion.where
  2.0 1.4 copy.10
  3.4 145.5 %layer.1 = (f32[128,2048]{1,0:T(8,128)}, bf16[3,32,64,128]{3,2,1,0:T(8,128)(2,1)}, f32[8,2048]{1,0:T(8,128)}) custom-call(s32[32,8]{1,0:T(8,128)} %bitcast.12, s32[32,32]{1,0:T(8,128)} %select_reduce_fusion.where, bf16[8,2048]{1,0:T(8,128)(2,1)} %weight.1, bf16[128,6144]{1,0:T(8,128)(2,1)} %bitcast.14, bf16[128,2048]{1,0:T(8,128)(2,1)} %bitcast.15, ...), custom_call_target="tpu_custom_call" | custom-call | flops 5368709120 | bytes 16777216 | tf_op jit(solution)/shard_map/layer/pallas_call | solution.py:507
  148.9 0.0 copy-start
  148.9 2.2 %convert_bitcast_fusion = bf16[1,128,2048]{2,1,0:T(8,128)(2,1)} fusion(f32[128,2048]{1,0:T(8,128)} %get-tuple-element.6), kind=kLoop, calls=%fused_computation | loop fusion | flops 262144 | bytes 1572864 | tf_op jit(solution)/shard_map/broadcast_in_dim | solution.py:563
  151.1 0.0 copy-done
  151.1 0.0 copy-start.1
  151.1 1.6 %copy.12 = bf16[6144,128]{0,1:T(8,128)(2,1)} copy(bf16[6144,128]{1,0:T(8,128)(2,1)S(1)} %bitcast.11) | data formatting | bytes 3145728 | tf_op jit(solution)/shard_map/reshape | solution.py:562
  152.7 0.0 copy-done.1
  152.7 0.6 copy.15
  (1 shorter events, 0.0 us)
Async XLA Ops:
  148.9 2.2 %copy-start = (bf16[3,32,64,128]{3,2,1,0:T(8,128)(2,1)S(1)}, bf16[3,32,64,128]{3,2,1,0:T(8,128)(2,1)}, u32[]{:S(2)}) copy-start(bf16[3,32,64,128]{3,2,1,0:T(8,128)(2,1)} %get-tuple-element.7) | copy-start | bytes 4718596
  151.1 1.6 %copy-start.1 = (f32[8,2048]{1,0:T(8,128)S(1)}, f32[8,2048]{1,0:T(8,128)}, u32[]{:S(2)}) copy-start(f32[8,2048]{1,0:T(8,128)} %get-tuple-element.14) | copy-start | bytes 196612

commit v7 on v6

--- a/solution.py
+++ b/solution.py
@@ -27,7 +27,7 @@
 def layer_kernel(
     layout, where, weight, rows_in, upstream_in, mask_in, attended, pieces, weight_grad,
     qkv, grad, grads, run_weight, rows, upstream, mask, turned, sent, mixed, full_weight,
-    kvn, parts, probs, scores, out, context, swapped, partial, across, along,
+    kvn, parts, probs, slopes, scores, out, context, swapped, partial, across, along,
     in_sem, w_send, w_recv, m_send, m_recv, q_send, q_recv, x_send, x_recv, g_send, g_recv,
     f_send, f_recv, c_send, c_recv, b_send, b_recv, k_send, k_recv,
     s_send, s_recv, a_send, a_recv, l_send, l_recv,
@@ -223,7 +223,7 @@
     lax.fori_loop(0, seq - 1, arrive_qkv, 0)
 
     blocks, length = heads, tokens
-    picks = layout.shape[1]
+    picks = layout.shape[0]
     pair = 2 * head
     eighths = length // 8
 
@@ -234,58 +234,64 @@
     lax.fori_loop(0, blocks, prepare, 0, unroll=4)
     parts[blocks * picks] = jnp.zeros((length, pair), jnp.float32)
 
-    def arrive_grad(k, carry):
-        head_copy(k).wait_recv()
-        return carry
-
-    lax.fori_loop(0, seq - 1, arrive_grad, 0)
     low = lax.broadcasted_iota(jnp.int32, (length, pair), 1) < head
 
     def picked(r):
-        return [layout[r, j] for j in range(picks)]
-
-    def scores_of(r, slot):
-        q = qkv[r, 0] * jnp.bfloat16(SCALE)
-        g = grad[r]
-        none = jnp.zeros_like(q)
-        into = jnp.concatenate([jnp.concatenate([q, none], 1), jnp.concatenate([none, g], 1)], 0)
+        return [layout[j, r] for j in range(picks)]
+
+    def row(k):
+        return shifted(z, y, k)
+
+    def scores_of(k, slot):
+        q = qkv[row(k), 0] * jnp.bfloat16(SCALE)
+        into = jnp.concatenate([q, jnp.zeros_like(q)], 0)
         top = None
-        for j, b in enumerate(picked(r)):
-            both = jnp.dot(kvn[b], into, preferred_element_type=jnp.float32)
-            scores[slot, j] = both
-            part = jnp.max(both[:, :length].reshape(eighths, 8, length), axis=0)
+        for j, b in enumerate(picked(row(k))):
+            score = jnp.dot(kvn[b], into, preferred_element_type=jnp.float32)
+            scores[slot, j] = score
+            part = jnp.max(score.reshape(eighths, 8, length), axis=0)
             top = part if top is None else jnp.maximum(top, part)
         return jnp.max(top, axis=0, keepdims=True)
 
-    def probs_of(slot, top):
+    def probs_of(k, slot, top):
         total = jnp.zeros((8, length), jnp.float32)
-        delta = jnp.zeros((8, length), jnp.float32)
         for j in range(picks):
-            e = jnp.exp(scores[slot, j, :, :length] - top)
-            scores[slot, j, :, :length] = e
+            e = jnp.exp(scores[slot, j] - top)
+            scores[slot, j] = e
             total += jnp.sum(e.reshape(eighths, 8, length), axis=0)
-            delta += jnp.sum((e * scores[slot, j, :, length:]).reshape(eighths, 8, length), axis=0)
         inverse = 1.0 / jnp.sum(total, axis=0, keepdims=True)
-        delta = jnp.sum(delta, axis=0, keepdims=True) * inverse
         for j in range(picks):
-            p = scores[slot, j, :, :length] * inverse
-            d = p * (scores[slot, j, :, length:] - delta)
+            probs[k, pl.ds(j * length, length)] = (scores[slot, j] * inverse).astype(jnp.bfloat16)
+
+    def context_of(k):
+        values = jnp.concatenate([qkv[b, 2] for b in picked(row(k))], 1)
+        out[row(k), 0] = jnp.dot(
+            values, probs[k], preferred_element_type=jnp.float32
+        ).astype(jnp.bfloat16)
+
+    def slopes_of(k, slot):
+        g = grad[row(k)]
+        into = jnp.concatenate([jnp.zeros_like(g), g], 0)
+        delta = jnp.sum(
+            g.astype(jnp.float32) * out[row(k), 0].astype(jnp.float32), axis=0, keepdims=True
+        )
+        for j, b in enumerate(picked(row(k))):
             rows = pl.ds(j * length, length)
-            probs[slot, rows, :length] = d.astype(jnp.bfloat16)
-            probs[slot, rows, length:] = p.astype(jnp.bfloat16)
-
-    def results_of(r, slot):
-        at = picked(r)
-        kvt = jnp.concatenate([qkv[b, 1:3].reshape(pair, length) for b in at], 1)
-        both = jnp.dot(kvt, probs[slot], preferred_element_type=jnp.float32)
-        out[r, 0] = both[head:, length:].astype(jnp.bfloat16)
-        out[r, 1] = (both[:head, :length] * SCALE).astype(jnp.bfloat16)
+            slope = jnp.dot(kvn[b], into, preferred_element_type=jnp.float32) - delta
+            slope = probs[k, rows].astype(jnp.float32) * slope
+            slopes[slot, rows] = slope.astype(jnp.bfloat16)
+
+    def results_of(k, slot):
+        r = row(k)
+        keys = jnp.concatenate([qkv[b, 1] for b in picked(r)], 1)
+        value = jnp.dot(keys, slopes[slot], preferred_element_type=jnp.float32)
+        out[r, 1] = (value * SCALE).astype(jnp.bfloat16)
         turned = jnp.concatenate([qkv[r, 0] * jnp.bfloat16(SCALE), grad[r]], 0).T
         into = jnp.concatenate([jnp.where(low, turned, 0), jnp.where(low, 0, turned)], 0)
         for j in range(picks):
-            parts[r * picks + j] = jnp.dot(
-                probs[slot, pl.ds(j * length, length), :], into, preferred_element_type=jnp.float32
-            )
+            rows = pl.ds(j * length, length)
+            both = jnp.concatenate([slopes[slot, rows], probs[k, rows]], 1)
+            parts[r * picks + j] = jnp.dot(both, into, preferred_element_type=jnp.float32)
 
     def context_copy(k):
         peer = shifted(z, y, k)
@@ -305,32 +311,47 @@
             out.at[peer, pl.ds(2, 2)], pieces.at[pl.ds(1, 2), s], k_send.at[k], k_recv.at[k], **to(d, peer)
         )
 
-    def row(k):
-        return shifted(z, y, k)
-
-    def give(k, slot):
-        results_of(row(k), slot)
+    def give_context(k):
+        context_of(k)
         context_copy(k).start()
+
+    probs_of(0, 0, scores_of(0, 0))
+
+    def two_forward(i, top):
+        k = 2 * i
+        later = scores_of(k + 2, 0)
+        give_context(k)
+        probs_of(k + 1, 1, top)
+        last = scores_of(k + 3, 1)
+        give_context(k + 1)
+        probs_of(k + 2, 0, later)
+        return last
+
+    top = lax.fori_loop(0, blocks // 2 - 1, two_forward, scores_of(1, 1))
+    give_context(blocks - 2)
+    probs_of(blocks - 1, 1, top)
+    context_of(blocks - 1)
+    context[s] = out[s, 0]
+
+    def arrive_grad(k, carry):
+        head_copy(k).wait_recv()
+        return carry
+
+    lax.fori_loop(0, seq - 1, arrive_grad, 0)
+    def give_query(k, slot):
+        results_of(k, slot)
         query_copy(k).start()
 
-    probs_of(0, scores_of(row(0), 0))
-
-    def two_rows(i, top):
+    def two_backward(i, carry):
         k = 2 * i
-        later = scores_of(row(k + 2), 0)
-        give(k, 0)
-        probs_of(1, top)
-        last = scores_of(row(k + 3), 1)
-        give(k + 1, 1)
-        probs_of(0, later)
-        return last
-
-    top = lax.fori_loop(0, blocks // 2 - 1, two_rows, scores_of(row(1), 1))
-    give(blocks - 2, 0)
-    probs_of(1, top)
-    results_of(s, 1)
-    context[s] = out[s, 0]
-    pieces[0, s] = out[s, 1]
+        slopes_of(k + 1, 1)
+        give_query(k, 0)
+        slopes_of(k + 2, 0)
+        give_query(k + 1, 1)
+        return carry
+
+    slopes_of(0, 0)
+    lax.fori_loop(0, blocks // 4, two_backward, 0)
 
     def wait_context(k, carry):
         context_copy(k).wait_recv()
@@ -350,21 +371,11 @@
 
     lax.fori_loop(1, runs, send_swap, 0)
     swapped[d] = context[pl.ds(d * group, group)]
-
-    def keys_of(u):
-        total = parts[where[u, 0]]
-        for r in range(1, blocks):
-            total += parts[where[u, r]]
-        out[u, 2:4] = total.T.astype(jnp.bfloat16).reshape(2, head, length)
-
-    def give_keys(k, carry):
-        keys_of(row(k))
-        key_copy(k).start()
-        return carry
-
-    lax.fori_loop(0, seq - 1, give_keys, 0)
-    keys_of(s)
-    pieces[1:3, s] = out[s, 2:4]
+    lax.fori_loop(blocks // 4, blocks // 2 - 1, two_backward, 0)
+    slopes_of(blocks - 1, 1)
+    give_query(blocks - 2, 0)
+    results_of(blocks - 1, 1)
+    pieces[0, s] = out[s, 1]
 
     def wait_swap(k, carry):
         swap_copy(k).wait_recv()
@@ -394,6 +405,21 @@
     for k in range(1, 4):
         across_copy(k).start()
 
+    def keys_of(u):
+        total = parts[where[u, 0]]
+        for r in range(1, blocks):
+            total += parts[where[u, r]]
+        out[u, 2:4] = total.T.astype(jnp.bfloat16).reshape(2, head, length)
+
+    def give_keys(k, carry):
+        keys_of(row(k))
+        key_copy(k).start()
+        return carry
+
+    lax.fori_loop(0, seq - 1, give_keys, 0)
+    keys_of(s)
+    pieces[1:3, s] = out[s, 2:4]
+
     def attend(run, rows):
         left = context[pl.ds(run * group, group)].reshape(share, tokens).T
         return jnp.dot(left, rows, preferred_element_type=jnp.float32)
@@ -411,8 +437,6 @@
         attended[...] += attend(run, full_weight[run])
         return carry
 
-    attended[...] = attend(d, run_weight[...])
-    lax.fori_loop(1, 4, full_near, 0)
 
     for k in range(1, 4):
         across_copy(k).wait_recv()
@@ -436,6 +460,8 @@
 
     lax.fori_loop(0, 8, add_across, 0)
     lax.fori_loop(1, 8, send_along, 0)
+    attended[...] = attend(d, run_weight[...])
+    lax.fori_loop(1, 4, full_near, 0)
     lax.fori_loop(0, 4, full_other, 0)
 
     def wait_along(k, carry):
@@ -498,7 +524,7 @@
 
 def layer(layout, where, weight, rows, upstream, mask, runs):
     tokens, model = upstream.shape
-    heads, picks = layout.shape
+    picks, heads = layout.shape
     depth = weight.shape[0]
     group = heads // runs
     bf16, f32, dma = jnp.bfloat16, jnp.float32, pltpu.SemaphoreType.DMA
@@ -528,8 +554,9 @@
             pltpu.VMEM((runs, heads * depth, model), bf16),
             pltpu.VMEM((heads, tokens, 2 * HS), bf16),
             pltpu.VMEM((heads * picks + 1, tokens, 2 * HS), f32),
-            pltpu.VMEM((2, picks * tokens, 2 * tokens), bf16),
-            pltpu.VMEM((2, picks, tokens, 2 * tokens), f32),
+            pltpu.VMEM((heads, picks * tokens, tokens), bf16),
+            pltpu.VMEM((2, picks * tokens, tokens), bf16),
+            pltpu.VMEM((2, picks, tokens, tokens), f32),
             pltpu.VMEM((heads, 4, HS, tokens), bf16),
             pltpu.VMEM((heads, HS, tokens), bf16),
             pltpu.VMEM((runs, group, HS, tokens), bf16),
@@ -544,18 +571,18 @@
             flops=20 * heads * tokens * picks * tokens * HS, bytes_accessed=16 << 20, transcendentals=0
         ),
         compiler_params=pltpu.CompilerParams(
-            collective_id=0, has_side_effects=True, vmem_limit_bytes=58 << 20
+            collective_id=0, has_side_effects=True, vmem_limit_bytes=60 << 20
         ),
     )(layout, where, weight, rows, upstream, mask)
 
 
 def on_device(projected, out_weight, upstream, peak_mask, block_layout):
     inner = projected.shape[2] // 3
-    layout = block_layout[0]
-    blocks, picks = layout.shape
-    index = jnp.arange(blocks * picks, dtype=jnp.int32).reshape(1, blocks, picks)
-    same = layout[None] == jnp.arange(blocks, dtype=jnp.int32)[:, None, None]
-    where = jnp.min(jnp.where(same, index, blocks * picks), axis=2)
+    layout = block_layout[0].T
+    picks, blocks = layout.shape
+    index = jnp.arange(picks)[:, None] + picks * jnp.arange(blocks)
+    same = layout[:, None] == jnp.arange(blocks)[None, :, None]
+    where = jnp.min(jnp.where(same, index[:, None], blocks * picks), axis=0).astype(jnp.int32)
     attended, projected_grad, weight_grad = layer(
         layout, where, out_weight, projected[0], upstream[0], peak_mask, lax.axis_size("dp")
     )

time: 154 us -> 148 us (0.961)
  the two profiles are of different devices: /device:TPU:38 before, /device:TPU:1 now
where the time goes in v7:
time: 148 us
  Pallas kernels  141 us (95%)
  other arithmetic  3.53 us (2%)
  local copies, waits for them, and re-layouts  2.2 us (1%)
    pallas_call x1, Pallas kernels, layer(): pl.pallas_call(layer_kernel, name='layer', out_shape=(jax.ShapeDtypeStruc...  141 us

profile of v7, /device:TPU:1, one launch (start us, length us, event | category | flops | bytes accessed | tf_op | source)
XLA Modules:
  0.0 147.5 jit_solution(11518416576147818839)
XLA Ops:
  0.7 1.3 select_reduce_fusion.where
  2.0 141.1 %layer.1 = (f32[128,2048]{1,0:T(8,128)}, bf16[3,32,64,128]{3,2,1,0:T(8,128)(2,1)}, f32[8,2048]{1,0:T(8,128)}) custom-call(s32[8,32]{1,0:T(8,128)} %bitcast.14, s32[32,32]{1,0:T(8,128)} %select_reduce_fusion.where, bf16[8,2048]{1,0:T(8,128)(2,1)} %weight.1, bf16[128,6144]{1,0:T(8,128)(2,1)} %bitcast.15, bf16[128,2048]{1,0:T(8,128)(2,1)} %bitcast.16, ...), custom_call_target="tpu_custom_call" | custom-call | flops 5368709120 | bytes 16777216 | tf_op jit(solution)/shard_map/layer/pallas_call | solution.py:533
  143.1 0.0 copy-start
  143.1 2.2 %convert_bitcast_fusion = bf16[1,128,2048]{2,1,0:T(8,128)(2,1)} fusion(f32[128,2048]{1,0:T(8,128)} %get-tuple-element.6), kind=kLoop, calls=%fused_computation | loop fusion | flops 262144 | bytes 1572864 | tf_op jit(solution)/shard_map/broadcast_in_dim | solution.py:590
  145.3 0.0 copy-done
  145.3 0.0 copy-start.1
  145.3 1.6 %copy.9 = bf16[6144,128]{0,1:T(8,128)(2,1)} copy(bf16[6144,128]{1,0:T(8,128)(2,1)S(1)} %bitcast.12) | data formatting | bytes 3145728 | tf_op jit(solution)/shard_map/reshape | solution.py:589
  146.9 0.0 copy-done.1
  146.9 0.6 copy.11
  (2 shorter events, 0.0 us)
Async XLA Ops:
  143.1 2.2 %copy-start = (bf16[3,32,64,128]{3,2,1,0:T(8,128)(2,1)S(1)}, bf16[3,32,64,128]{3,2,1,0:T(8,128)(2,1)}, u32[]{:S(2)}) copy-start(bf16[3,32,64,128]{3,2,1,0:T(8,128)(2,1)} %get-tuple-element.7) | copy-start | bytes 4718596
  145.3 1.6 %copy-start.1 = (f32[8,2048]{1,0:T(8,128)S(1)}, f32[8,2048]{1,0:T(8,128)}, u32[]{:S(2)}) copy-start(f32[8,2048]{1,0:T(8,128)} %get-tuple-element.14) | copy-start | bytes 196612

commit v8 on v7

--- a/solution.py
+++ b/solution.py
@@ -438,6 +438,8 @@
         return carry
 
 
+    attended[...] = attend(d, run_weight[...])
+    lax.fori_loop(1, 4, full_near, 0)
     for k in range(1, 4):
         across_copy(k).wait_recv()
 
@@ -460,8 +462,6 @@
 
     lax.fori_loop(0, 8, add_across, 0)
     lax.fori_loop(1, 8, send_along, 0)
-    attended[...] = attend(d, run_weight[...])
-    lax.fori_loop(1, 4, full_near, 0)
     lax.fori_loop(0, 4, full_other, 0)
 
     def wait_along(k, carry):

time: 148 us -> 148 us (level)
  no operation moved by 1% of the time
where the time goes in v8:
time: 148 us
  Pallas kernels  141 us (95%)
  other arithmetic  3.53 us (2%)
  local copies, waits for them, and re-layouts  2.2 us (1%)
    pallas_call x1, Pallas kernels, layer(): pl.pallas_call(layer_kernel, name='layer', out_shape=(jax.ShapeDtypeStruc...  141 us

profile of v8, /device:TPU:1, one launch (start us, length us, event | category | flops | bytes accessed | tf_op | source)
XLA Modules:
  0.0 147.5 jit_solution(4719977023323563609)
XLA Ops:
  0.7 1.3 select_reduce_fusion.where
  2.0 141.1 %layer.1 = (f32[128,2048]{1,0:T(8,128)}, bf16[3,32,64,128]{3,2,1,0:T(8,128)(2,1)}, f32[8,2048]{1,0:T(8,128)}) custom-call(s32[8,32]{1,0:T(8,128)} %bitcast.14, s32[32,32]{1,0:T(8,128)} %select_reduce_fusion.where, bf16[8,2048]{1,0:T(8,128)(2,1)} %weight.1, bf16[128,6144]{1,0:T(8,128)(2,1)} %bitcast.15, bf16[128,2048]{1,0:T(8,128)(2,1)} %bitcast.16, ...), custom_call_target="tpu_custom_call" | custom-call | flops 5368709120 | bytes 16777216 | tf_op jit(solution)/shard_map/layer/pallas_call | solution.py:533
  143.1 0.0 copy-start
  143.1 2.2 %convert_bitcast_fusion = bf16[1,128,2048]{2,1,0:T(8,128)(2,1)} fusion(f32[128,2048]{1,0:T(8,128)} %get-tuple-element.6), kind=kLoop, calls=%fused_computation | loop fusion | flops 262144 | bytes 1572864 | tf_op jit(solution)/shard_map/broadcast_in_dim | solution.py:590
  145.3 0.0 copy-done
  145.3 0.0 copy-start.1
  145.3 1.6 %copy.9 = bf16[6144,128]{0,1:T(8,128)(2,1)} copy(bf16[6144,128]{1,0:T(8,128)(2,1)S(1)} %bitcast.12) | data formatting | bytes 3145728 | tf_op jit(solution)/shard_map/reshape | solution.py:589
  146.9 0.0 copy-done.1
  146.9 0.6 copy.11
  (2 shorter events, 0.0 us)
Async XLA Ops:
  143.1 2.2 %copy-start = (bf16[3,32,64,128]{3,2,1,0:T(8,128)(2,1)S(1)}, bf16[3,32,64,128]{3,2,1,0:T(8,128)(2,1)}, u32[]{:S(2)}) copy-start(bf16[3,32,64,128]{3,2,1,0:T(8,128)(2,1)} %get-tuple-element.7) | copy-start | bytes 4718596
  145.3 1.6 %copy-start.1 = (f32[8,2048]{1,0:T(8,128)S(1)}, f32[8,2048]{1,0:T(8,128)}, u32[]{:S(2)}) copy-start(f32[8,2048]{1,0:T(8,128)} %get-tuple-element.14) | copy-start | bytes 196612
